TPU v7x, 256 devices: a whole 4x4x8 slice. The times are simulated.
256 devices in a mesh: space: 32 (over y, z), spec: 8 (over x, core).
Axes of the slice: x: 4, y: 4, z: 8, core: 2. Of those that a mesh axis runs over, the one named last changes fastest.
Arguments:
- spectra: float32 [1296, 32768], P('spec', 'space'), may hold values from 0.1 to 2
- wet_mask: int32 [32768], P('space'), may hold values 0 or 1
- depth_class: int32 [32768], P('space'), may hold values from 0 to 31
- cg_table: float32 [36, 32], replicated, may hold values from 0.3 to 1
- neighbour: int32 [8, 32768], P(None, 'space'), may hold values from 0 to 3071, as said below
- edge_weight: float32 [8, 32768], P(None, 'space'), may hold values from 0.02 to 0.11
- edge_angle: float32 [8, 32768], P(None, 'space'), may hold values from -3.140625 to 3.140625
- send_list: int32 [32, 32, 64], P('space'), may hold values from 0 to 1023, as said below
- friction: float32 [32768], P('space'), may hold values from 0.2 to 1.5
- wind_dir: float32 [32768], P('space'), may hold values from -3.140625 to 3.140625
Outputs:
- spectra_next: float32 [1296, 32768], P('spec', 'space')
- energy: float32 [32768], P(('space', 'spec'))
Inputs may be any that keep to these rules, and one draw needn't show every extreme that they name: `send_list`: block s sends only to blocks (s + 1), (s - 1), (s + 2), (s - 2) and (s + 16), all modulo 32; entries of any other pair, and entries at or past a pair's used count, are 0. The pair from each block s to block (s + 1) % 32 uses all 64 slots and its slot 0 holds node 1023. `neighbour`: A ghost entry 1024 + p * 64 + g has p among the blocks that send to the node's block and g below the count that block p uses towards it; an unused slot holds the node's own local index. Node 0 of every block b has slot 0 at ghost slot 63 from block (b - 1) % 32.
All inputs are finite; a program needn't handle non-finite values. No bound on the sum of `wet_mask` on one device may be relied on, other than what follows from the above.
Results may differ from a plain program's by a relative error of at most 0.000067.
Values sent between devices are 32-bit elements; how exact they have to be, the bound alone decides.
No kernel may reach another device: no remote copies, remote signals or barrier semaphores. Data moves between devices by JAX's collectives and lax.ppermute only.
A program may use at most 64 MiB of HBM per device.

v0:
```python
import math

import jax
import jax.numpy as jnp
from jax import lax
from jax.sharding import PartitionSpec as P

NDIR = 36
NFREQ = 36
NCLASS = 32


def spectral_constants():
    level_index = jnp.arange(NFREQ, dtype=jnp.float32)
    frequency = 0.04 * jnp.exp(level_index * jnp.float32(math.log(1.1)))
    spread = 0.1 * frequency
    band_weight = spread / (NDIR * jnp.sum(spread))
    direction_angle = jnp.arange(NDIR, dtype=jnp.float32) * jnp.float32(2.0 * math.pi / NDIR)
    return (frequency, band_weight, jnp.cos(direction_angle), jnp.sin(direction_angle))


def point_source(values, energy, moment, freq_col, cos_col, sin_col, friction_row, dir_row):
    top_freq = 0.04 * jnp.exp(jnp.float32(NFREQ - 1) * jnp.float32(math.log(1.1)))
    mean_freq = (moment + 4e-08) / (energy + 1e-06)
    steepness = energy * (mean_freq / 0.8) ** 4
    dissipation = (steepness**2)[None, :] * freq_col[:, None] / mean_freq[None, :]
    drive = (
        cos_col[:, None] * jnp.cos(dir_row)[None, :] + sin_col[:, None] * jnp.sin(dir_row)[None, :]
    )
    relative = freq_col / top_freq
    wind_input = 0.5 * jnp.maximum(
        4.0 * friction_row[None, :] * relative[:, None] * drive - 1.0, 0.0
    )
    return values * jnp.exp(0.25 * (wind_input - dissipation))


def per_device(
    spectra,
    wet_mask,
    depth_class,
    cg_table,
    neighbour,
    edge_weight,
    edge_angle,
    send_list,
    friction,
    wind_dir,
):
    comp_count, node_count = spectra.shape
    spec_count = lax.axis_size("spec")
    slot_count = neighbour.shape[0]
    frequency, band_weight, dir_cosine, dir_sine = spectral_constants()
    comp_range = lax.axis_index("spec") * comp_count + jnp.arange(comp_count, dtype=jnp.int32)
    freq_index = comp_range // NDIR
    dir_index = comp_range % NDIR
    cos_col = dir_cosine[dir_index]
    sin_col = dir_sine[dir_index]
    wet_float = wet_mask.astype(jnp.float32)
    masked = spectra * wet_float[None, :]
    outgoing = jnp.take(masked, send_list[0].reshape(-1), axis=1)
    ghost_values = lax.all_to_all(outgoing, "space", split_axis=1, concat_axis=1, tiled=True)
    class_hits = (jnp.arange(NCLASS, dtype=jnp.int32)[:, None] == depth_class[None, :]).astype(
        jnp.float32
    )
    group_speed = jnp.dot(
        cg_table[freq_index],
        class_hits,
        precision=lax.Precision.HIGHEST,
        preferred_element_type=jnp.float32,
    )
    accumulated = jnp.zeros_like(masked)
    extended = jnp.concatenate([masked, ghost_values], axis=1)
    gathered_all = jnp.take(extended, neighbour.reshape(-1), axis=1)
    for slot_index in range(slot_count):
        gathered = gathered_all[:, slot_index * node_count : (slot_index + 1) * node_count]
        alignment = (
            cos_col[:, None] * jnp.cos(edge_angle[slot_index])[None, :]
            + sin_col[:, None] * jnp.sin(edge_angle[slot_index])[None, :]
        )
        accumulated = accumulated + group_speed * edge_weight[slot_index][None, :] * jnp.maximum(
            alignment, 0.0
        ) * (gathered - masked)
    advected = (masked + accumulated) * wet_float[None, :]
    point_count = node_count // spec_count
    offset = lax.axis_index("spec") * point_count
    blocked = advected.reshape(comp_count, spec_count, point_count)
    gathered_points = lax.all_to_all(
        blocked, "spec", split_axis=1, concat_axis=0, tiled=True
    ).reshape(comp_count * spec_count, point_count)
    full_range = jnp.arange(comp_count * spec_count, dtype=jnp.int32)
    full_freq = full_range // NDIR
    full_dir = full_range % NDIR
    freq_col = frequency[full_freq]
    weight_col = band_weight[full_freq]
    energy = jnp.sum(gathered_points * weight_col[:, None], axis=0)
    moment = jnp.sum(gathered_points * (weight_col * freq_col)[:, None], axis=0)
    friction_part = lax.dynamic_slice_in_dim(friction, offset, point_count)
    wind_part = lax.dynamic_slice_in_dim(wind_dir, offset, point_count)
    updated = point_source(
        gathered_points,
        energy,
        moment,
        freq_col,
        dir_cosine[full_dir],
        dir_sine[full_dir],
        friction_part,
        wind_part,
    )
    returned = lax.all_to_all(
        updated.reshape(comp_count * spec_count, 1, point_count),
        "spec",
        split_axis=0,
        concat_axis=1,
        tiled=True,
    )
    return (returned.reshape(comp_count, node_count), energy)


def solution(mesh):
    placed = (
        P("spec", "space"),
        P("space"),
        P("space"),
        P(),
        P(None, "space"),
        P(None, "space"),
        P(None, "space"),
        P("space", None, None),
        P("space"),
        P("space"),
    )
    return jax.shard_map(
        per_device,
        mesh=mesh,
        in_specs=placed,
        out_specs=(P("spec", "space"), P(("space", "spec"))),
        check_vma=False,
    )
```

profile of v0, /device:TPU:1, one launch (start us, length us, event | category | flops | bytes accessed | tf_op | source)
XLA Modules:
  0.0 211.6 jit_solution(6362153186703250153)
XLA Ops:
  0.6 0.8 reshape_squeeze.6
  2.8 1.2 broadcast_multiply_fusion
  4.4 6.6 %gather_fusion.3 = f32[2048,162]{1,0:T(8,128)S(1)} fusion(f32[162,1024]{0,1:T(8,128)S(1)} %copy.29, s32[2048]{0:T(1024)S(1)} %broadcast_clamp_fusion.1), kind=kCustom, calls=%fused_computation.3 | custom fusion | bytes 2662400 | tf_op jit(solution)/shard_map/jit(_take)/gather | solution.py:60
  11.0 1.7 broadcast_select_fusion
  12.7 12.2 %all-to-all-start = ((f32[162,32,64]{0,2,1:T(8,128)}), f32[162,32,64]{0,2,1:T(8,128)S(1)}, u32[]{:S(2)}, u32[]{:S(2)}) async-start(f32[162,32,64]{0,2,1:T(8,128)} %broadcast_select_fusion), calls=%async_computation | async-start | bytes 4194304 | tf_op jit(solution)/shard_map/all_to_all | solution.py:61
  28.8 0.7 fusion.35
  33.0 0.7 fusion.32
  34.5 1.6 gather_fusion.2
  36.1 1.6 gather_fusion.1
  39.2 0.8 dynamic-slice_cosine_fusion
  40.0 4.5 %fusion.18 = f32[1296]{0:T(1024)S(1)} fusion(f32[]{:T(128)} %bitcast.173, f32[]{:T(128)} %bitcast.174, f32[]{:T(128)} %bitcast.175, f32[]{:T(128)} %bitcast.176, f32[]{:T(128)} %bitcast.177, f32[]{:T(128)} %bitcast.179, f32[]{:T(128)} %bitcast.178), kind=kLoop, calls=%fused_computation.142 | loop fusion | flops 29808 | bytes 5212 | tf_op jit(solution)/shard_map/gather | solution.py:94
  44.5 4.3 %fusion.19 = f32[1296]{0:T(1024)S(1)} fusion(f32[]{:T(128)} %bitcast.64, f32[]{:T(128)} %bitcast.65, f32[]{:T(128)} %bitcast.66, f32[]{:T(128)} %bitcast.67, f32[]{:T(128)} %bitcast.68, f32[]{:T(128)} %bitcast.70, f32[]{:T(128)} %bitcast.69), kind=kLoop, calls=%fused_computation.143 | loop fusion | flops 29808 | bytes 5212 | tf_op jit(solution)/shard_map/gather | solution.py:93
  48.8 4.3 %fusion.20 = f32[1296]{0:T(1024)S(1)} fusion(f32[]{:T(128)} %bitcast.136, f32[]{:T(128)} %bitcast.137, f32[]{:T(128)} %bitcast.138, f32[]{:T(128)} %bitcast.139, f32[]{:T(128)} %bitcast.140, f32[]{:T(128)} %bitcast.142, f32[]{:T(128)} %bitcast.141), kind=kLoop, calls=%fused_computation.144 | loop fusion | flops 27216 | bytes 5212 | tf_op jit(solution)/shard_map/gather | solution.py:105
  53.2 17.8 %select_select_fusion = f32[1296]{0:T(1024)S(1)} fusion(pred[1296]{0:T(1024)(128)(4,1)S(1)} %compare_reduce_fusion.29, pred[1296]{0:T(1024)(128)(4,1)S(1)} %compare_reduce_fusion.30, pred[1296]{0:T(1024)(128)(4,1)S(1)} %compare_reduce_fusion.31, pred[1296]{0:T(1024)(128)(4,1)S(1)} %compare_reduce_fusion.32, pred[1296]{0:T(1024)(128)(4,1)S(1)} %compare_reduce_fusion.33, ...), kind=kLoop, calls=%fused_computation.136 | loop fusion | flops 37584 | bytes 48068 | tf_op jit(solution)/shard_map/gather | solution.py:94
  71.1 18.0 %broadcast_multiply_fusion.1 = (f32[1296]{0:T(1024)S(1)}, f32[1296]{0:T(1024)S(1)}) fusion(pred[1296]{0:T(1024)(128)(4,1)S(1)} %compare_reduce_fusion.29, pred[1296]{0:T(1024)(128)(4,1)S(1)} %compare_reduce_fusion.30, pred[1296]{0:T(1024)(128)(4,1)S(1)} %compare_reduce_fusion.31, pred[1296]{0:T(1024)(128)(4,1)S(1)} %compare_reduce_fusion.32, ...), kind=kLoop, calls=%fused_computation.149 | loop fusion | flops 38880 | bytes 53252 | tf_op jit(solution)/shard_map/div | solution.py:30
  89.1 1.0 slice_cosine_fusion.7
  90.1 1.3 copy-done.1
  91.5 2.1 pad_maximum_fusion
  93.5 31.4 %gather_fusion.4 = f32[8192,162]{1,0:T(8,128)} fusion(f32[162,3072]{0,1:T(8,128)S(1)} %pad_maximum_fusion, s32[8192]{0:T(1024)S(1)} %broadcast_clamp_fusion), kind=kCustom, calls=%fused_computation.4 | custom fusion | bytes 10649600 | tf_op jit(solution)/shard_map/jit(_take)/gather | solution.py:73
  124.9 8.4 %copy.30 = f32[8192,162]{0,1:T(8,128)} copy(f32[8192,162]{1,0:T(8,128)} %gather_fusion.4) | data formatting | bytes 10616832 | tf_op jit(solution)/shard_map/jit(_take)/gather | solution.py:73
  133.3 3.1 %select_bitcast_fusion = f32[162,8192]{1,0:T(8,128)S(1)} fusion(f32[8192,162]{0,1:T(8,128)} %copy.30, pred[8192]{0:T(1024)(128)(4,1)S(1)} %compare_and_fusion), kind=kLoop, calls=%fused_computation.5 | loop fusion | flops 1327104 | bytes 10625024 | tf_op jit(solution)/shard_map/jit(_take)/select_n | solution.py:73
  136.4 2.4 %fusion.3 = f32[162,1024]{1,0:T(8,128)S(1)} fusion(f32[162,8192]{1,0:T(8,128)S(1)} %select_bitcast_fusion, f32[162,32]{1,0:T(8,128)S(1)} %gather_fusion, f32[1024]{0:T(1024)S(1)} %bitcast.243, f32[1024]{0:T(1024)S(1)} %bitcast.249, f32[1024]{0:T(1024)S(1)} %bitcast.233, f32[1024]{0:T(1024)S(1)} %bitcast.242, f32[1024]{0:T(1024)S(1)} %bitcast.250, ...), kind=kOutput, calls=%fused_computation.12 | convolution fusion | flops 76009472 | bytes 6764048 | tf_op jit(solution)/shard_map/dot_general | solution.py:65
  139.0 1.0 copy.31
  140.0 5.2 %all-to-all-start.1 = ((f32[162,8,128]{2,0,1:T(8,128)}), f32[162,8,128]{2,0,1:T(8,128)S(1)}, u32[]{:S(2)}, u32[]{:S(2)}) async-start(f32[162,8,128]{2,0,1:T(8,128)} %copy.31), calls=%async_computation.1 | async-start | bytes 1376256 | tf_op jit(solution)/shard_map/all_to_all | solution.py:87
  145.5 4.6 %fusion.21 = f32[1296]{0:T(1024)S(1)} fusion(f32[]{:T(128)} %bitcast.100, f32[]{:T(128)} %bitcast.101, f32[]{:T(128)} %bitcast.102, f32[]{:T(128)} %bitcast.103, f32[]{:T(128)} %bitcast.104, f32[]{:T(128)} %bitcast.106, f32[]{:T(128)} %bitcast.105), kind=kLoop, calls=%fused_computation.145 | loop fusion | flops 27216 | bytes 5212 | tf_op jit(solution)/shard_map/gather | solution.py:104
  150.0 0.7 fusion.29
  150.8 18.1 %select_select_fusion.1 = f32[1296]{0:T(1024)S(1)} fusion(pred[1296]{0:T(1024)(128)(4,1)S(1)} %compare_reduce_fusion, pred[1296]{0:T(1024)(128)(4,1)S(1)} %compare_reduce_fusion.1, pred[1296]{0:T(1024)(128)(4,1)S(1)} %compare_reduce_fusion.2, pred[1296]{0:T(1024)(128)(4,1)S(1)} %compare_reduce_fusion.3, pred[1296]{0:T(1024)(128)(4,1)S(1)} %compare_reduce_fusion.4, ...), kind=kLoop, calls=%fused_computation.137 | loop fusion | flops 37584 | bytes 48068 | tf_op jit(solution)/shard_map/gather | solution.py:105
  168.9 18.2 %select_select_fusion.2 = f32[1296]{0:T(1024)S(1)} fusion(pred[1296]{0:T(1024)(128)(4,1)S(1)} %compare_reduce_fusion, pred[1296]{0:T(1024)(128)(4,1)S(1)} %compare_reduce_fusion.1, pred[1296]{0:T(1024)(128)(4,1)S(1)} %compare_reduce_fusion.2, pred[1296]{0:T(1024)(128)(4,1)S(1)} %compare_reduce_fusion.3, pred[1296]{0:T(1024)(128)(4,1)S(1)} %compare_reduce_fusion.4, ...), kind=kLoop, calls=%fused_computation.138 | loop fusion | flops 37584 | bytes 48068 | tf_op jit(solution)/shard_map/gather | solution.py:104
  187.6 1.1 exponential_multiply_fusion
  188.7 15.6 %all_to_all.39 = f32[1296,1,128]{2,1,0:T(1,128)S(1)} all-to-all(f32[1296,1,128]{2,1,0:T(1,128)S(1)} %bitcast.218), channel_id=1, replica_groups=mesh['space'=32,'spec'=8] {'spec'}, dimensions={0} | all-to-all | bytes 1327104 | tf_op jit(solution)/shard_map/all_to_all | solution.py:109
  204.9 5.5 %reduce.129 = f32[1296,128]{1,0:T(8,128)S(1)} reduce(f32[1296,1,128]{2,1,0:T(1,128)S(1)} %all_to_all.39, f32[]{:T(128)} %broadcast.1224), dimensions={1}, to_apply=%all_to_all.33.reduce_sub_computation.3 | reduce | bytes 1327108 | tf_op jit(solution)/shard_map/all_to_all | solution.py:109
  210.6 1.0 copy.40
  (114 shorter events, 12.4 us)
Async XLA Ops:
  4.3 6.7 %copy-start = (f32[162,1024]{0,1:T(8,128)}, f32[162,1024]{0,1:T(8,128)S(1)}, u32[]{:S(2)}) copy-start(f32[162,1024]{0,1:T(8,128)S(1)} %copy.29) | copy-start | bytes 1990660
  12.7 25.6 %copy-start.3 = (s32[8,1024]{1,0:T(8,128)S(1)}, s32[8,1024]{1,0:T(8,128)}, u32[]{:S(2)}) copy-start(s32[8,1024]{1,0:T(8,128)} %param.14) | copy-start | bytes 98308
  12.7 25.7 %copy-start.6 = (f32[36,32]{0,1:T(8,128)S(1)}, f32[36,32]{0,1:T(8,128)}, u32[]{:S(2)}) copy-start(f32[36,32]{0,1:T(8,128)} %param.13) | copy-start | bytes 13828
  12.7 40.5 %copy-start.5 = (f32[8,1024]{1,0:T(8,128)S(1)}, f32[8,1024]{1,0:T(8,128)}, u32[]{:S(2)}) copy-start(f32[8,1024]{1,0:T(8,128)} %param.15) | copy-start | bytes 98308
  12.7 76.3 %copy-start.4 = (f32[8,1024]{1,0:T(8,128)S(1)}, f32[8,1024]{1,0:T(8,128)}, u32[]{:S(2)}) copy-start(f32[8,1024]{1,0:T(8,128)} %param.16) | copy-start | bytes 98308
  12.7 77.4 %all-to-all-start = ((f32[162,32,64]{0,2,1:T(8,128)}), f32[162,32,64]{0,2,1:T(8,128)S(1)}, u32[]{:S(2)}, u32[]{:S(2)}) async-start(f32[162,32,64]{0,2,1:T(8,128)} %broadcast_select_fusion), calls=%async_computation | async-start | bytes 4194304 | tf_op jit(solution)/shard_map/all_to_all | solution.py:61
  90.1 1.4 copy-start.1
  133.3 3.1 %copy-start.2 = (f32[162,1024]{1,0:T(8,128)S(1)}, f32[162,1024]{1,0:T(8,128)}, u32[]{:S(2)}) copy-start(f32[162,1024]{1,0:T(8,128)} %param.10) | copy-start | bytes 1990660
  133.3 3.1 %copy-start.8 = (s32[1024]{0:T(1024)S(1)}, s32[1024]{0:T(1024)}, u32[]{:S(2)}) copy-start(s32[1024]{0:T(1024)} %param.12) | copy-start | bytes 12292
  140.0 47.2 %all-to-all-start.1 = ((f32[162,8,128]{2,0,1:T(8,128)}), f32[162,8,128]{2,0,1:T(8,128)S(1)}, u32[]{:S(2)}, u32[]{:S(2)}) async-start(f32[162,8,128]{2,0,1:T(8,128)} %copy.31), calls=%async_computation.1 | async-start | bytes 1376256 | tf_op jit(solution)/shard_map/all_to_all | solution.py:87
  187.6 22.9 %copy-start.7 = (f32[128]{0:T(128)}, f32[128]{0:T(128)S(1)}, u32[]{:S(2)}) copy-start(f32[128]{0:T(128)S(1)} %get-tuple-element.3) | copy-start | bytes 1540
where the time goes:
time: 214 us; the launch traced here: 212 us
  other arithmetic  112 us (52%)
  local copies, waits for them, and re-layouts  62.7 us (29%)
  starting transfers between devices  17.4 us (8%)
  blocking collectives  15.6 us (7%)
  matrix products  2.4 us (1%)
    gather x2, local copies, waits for them, and re-layouts, per_device(): gathered_all = jnp.take(extended, neighbour.reshape(-1), axis=1)  39.8 us
    gather x31, other arithmetic, per_device(): dir_cosine[full_dir]  24.8 us
    gather x2, other arithmetic, per_device(): dir_sine[full_dir]  22.4 us
    gather x2, other arithmetic, per_device(): weight_col = band_weight[full_freq]  22.3 us
    div x1, other arithmetic, point_source(): relative = freq_col / top_freq  18 us
    all_to_all x1, blocking collectives, per_device(): lax.all_to_all(updated.reshape(comp_count * spec_count, 1, point_count),...  15.6 us
    all_to_all x1, starting transfers between devices, per_device(): lax.all_to_all(outgoing, 'space', split_axis=1, concat_axis=1, tiled=True)  12.2 us
    gather x1, local copies, waits for them, and re-layouts, per_device(): outgoing = jnp.take(masked, send_list[0].reshape(-1), axis=1)  6.64 us
  transfers between devices with their start and end apart: 2, of which 0 were waited for; matrix products, arithmetic and copies ran while one was open for 50% of the time, Pallas kernels for 0%

commit v1 on v0

v1 whole, which is shorter than its diff:
```python
import math

import numpy as np
import jax
import jax.numpy as jnp
from jax import lax
from jax.experimental import pallas as pl
from jax.experimental.pallas import tpu as pltpu
from jax.sharding import PartitionSpec as P

NDIR = 36
NFREQ = 36
GHOST = 64
LANES = 128
PACK = 88
OFFSETS = (1, 31, 2, 30, 16)
SCALE = 32767.5

_F = 0.04 * np.exp(np.arange(NFREQ) * math.log(1.1))
_KAPPA = float(0.1 / (NDIR * np.sum(0.1 * _F)))
_FTOP = float(_F[-1])


def _tables():
    angle = 2.0 * np.pi * (np.arange(72) % NDIR) / NDIR
    cosine = np.repeat(np.cos(angle)[:, None], LANES, 1)
    sine = np.repeat(np.sin(angle)[:, None], LANES, 1)
    freq = np.zeros((40, LANES))
    freq[:NFREQ] = _F[:, None]
    return np.concatenate([cosine, sine, freq]).astype(np.float32)


def lane_gather(values, index):
    return jnp.take_along_axis(values, index, axis=1, mode="promise_in_bounds")


def pick(blocks, index, bits):
    level = [lane_gather(block, index) for block in blocks]
    for bit in bits:
        level = [
            jnp.where(bit, level[i + 1], level[i]) if i + 1 < len(level) else level[i]
            for i in range(0, len(level), 2)
        ]
    return level[0]


def row8(row):
    return jnp.broadcast_to(row, (8, LANES))


def send_kernel(me_ref, x_ref, wet_ref, send_ref, out_ref):
    me = me_ref[0]
    rows = [send_ref[pl.ds((me + o) & 31, 1), :] for o in OFFSETS]
    lane = lax.broadcasted_iota(jnp.int32, (8, LANES), 1)
    low = lane < GHOST
    index = []
    for a, b in ((0, 1), (2, 3), (4, 4)):
        full = row8(jnp.concatenate([rows[a], rows[b]], axis=1))
        block = full >> 7
        index.append((full & 127, [(block & 1) == 1, (block & 2) == 2, (block & 4) == 4]))
    wet = [row8(wet_ref[b : b + 1, :].astype(jnp.float32)) for b in range(8)]

    def source(g):
        if g < 20:
            return [
                x_ref[8 * g : 8 * g + 8, LANES * b : LANES * b + LANES] * wet[b] for b in range(8)
            ]
        zero = jnp.zeros((6, LANES), jnp.float32)
        return [
            jnp.concatenate([x_ref[160:162, LANES * b : LANES * b + LANES], zero], axis=0) * wet[b]
            for b in range(8)
        ]

    for g in range(11):
        first = source(g)
        second = source(g + 11) if g < 10 else None
        for q in range(3):
            top = pick(first, *index[q])
            bottom = pick(second, *index[q]) if second is not None else jnp.zeros_like(top)
            if q < 2:
                out_ref[2 * q, 8 * g : 8 * g + 8, :] = jnp.where(low, top, pltpu.roll(bottom, 64, 1))
                out_ref[2 * q + 1, 8 * g : 8 * g + 8, :] = jnp.where(
                    low, pltpu.roll(top, 64, 1), bottom
                )
            else:
                out_ref[4, 8 * g : 8 * g + 8, :] = jnp.where(low, top, bottom)


def local_kernel(
    id_ref,
    x_ref,
    wet_ref,
    nb_ref,
    ew_ref,
    ea_ref,
    dc_ref,
    cg_ref,
    fr_ref,
    wd_ref,
    tab_ref,
    base_ref,
    gain_ref,
    xs_ref,
    wind_ref,
    fc_ref,
    geo_ref,
    code_ref,
    packed,
    cgx,
    wloc,
):
    me = id_ref[0]
    spec = id_ref[1]
    par = spec & 1
    first_freq = (9 * spec) >> 1
    sign = (1 - 2 * par).astype(jnp.float32)
    entry = nb_ref[...]
    ghost = entry >= 1024
    angle = ea_ref[...]
    weight = ew_ref[...] * (sign * (1.0 / SCALE))
    wc = weight * jnp.cos(angle)
    ws = weight * jnp.sin(angle)
    wloc[0] = jnp.where(ghost, 0.0, wc)
    wloc[1] = jnp.where(ghost, 0.0, ws)
    geo_ref[0] = jnp.where(ghost, wc, 0.0)
    geo_ref[1] = jnp.where(ghost, ws, 0.0)
    peer = (entry - 1024) >> 6
    off = (me - peer) & 31
    half = (off == 31) | (off == 30)
    block = jnp.where(off == 16, 2, jnp.where((off == 2) | (off == 30), 1, 0))
    code_ref[...] = (entry & 63) + jnp.where(half, 64, 0) + 128 * block
    cgpad = [None] * 5
    fpad = [None] * 5
    for j in range(5):
        line = cg_ref[pl.ds(first_freq + j, 1), :]
        cgpad[j] = row8(jnp.concatenate([line, line, line, line], axis=1))
        fpad[j] = row8(tab_ref[pl.ds(144 + first_freq + j, 1), :])
    for g in range(21):
        comp = lax.broadcasted_iota(jnp.int32, (8, LANES), 0) + 8 * g + 18 * par
        cv, fv = cgpad[0], fpad[0]
        for j in range(1, 5):
            if 8 * g + 7 + 18 >= 36 * j:
                later = comp >= 36 * j
                cv = jnp.where(later, cgpad[j], cv)
                fv = jnp.where(later, fpad[j], fv)
        cgx[8 * g : 8 * g + 8, :] = cv
        fc_ref[8 * g : 8 * g + 8, :] = fv
    for b in range(8):
        lanes = slice(LANES * b, LANES * b + LANES)
        wet = row8(wet_ref[b : b + 1, :].astype(jnp.float32)) * SCALE
        for g in range(20):
            xs_ref[8 * g : 8 * g + 8, lanes] = x_ref[8 * g : 8 * g + 8, lanes] * wet
        tail = jnp.concatenate([x_ref[160:162, lanes], jnp.zeros((6, LANES), jnp.float32)], axis=0)
        xs_ref[160:168, lanes] = tail * wet
        for g in range(11):
            top = (xs_ref[8 * g : 8 * g + 8, lanes] + 0.5).astype(jnp.int32) << 16
            if g < 10:
                top = top | (xs_ref[8 * g + 88 : 8 * g + 96, lanes] + 0.5).astype(jnp.int32)
            packed[8 * g : 8 * g + 8, lanes] = top

    def node_block(b, carry):
        lanes = pl.ds(pl.multiple_of(b * LANES, LANES), LANES)
        wet = row8(wet_ref[pl.ds(b, 1), :].astype(jnp.float32))
        cls = row8(dc_ref[pl.ds(b, 1), :])
        total = [jnp.zeros((8, LANES), jnp.float32) for _ in range(21)]
        for m in range(8):
            full = row8(nb_ref[m : m + 1, lanes])
            index = full & 127
            bits = [(full & 128) != 0, (full & 256) != 0, (full & 512) != 0]
            wc = row8(wloc[0, m : m + 1, lanes])
            ws = row8(wloc[1, m : m + 1, lanes])
            for g in range(11):
                word = pick(
                    [packed[8 * g : 8 * g + 8, LANES * s : LANES * s + LANES] for s in range(8)],
                    index,
                    bits,
                )
                for h, value in ((g, lax.shift_right_logical(word, 16)), (g + 11, word & 65535)):
                    if h > 20:
                        continue
                    r = 8 * (h % 9)
                    share = jnp.maximum(
                        tab_ref[r : r + 8, :] * wc + tab_ref[72 + r : 80 + r, :] * ws, 0.0
                    )
                    total[h] = total[h] + share * (
                        value.astype(jnp.float32) - xs_ref[8 * h : 8 * h + 8, lanes]
                    )
        drive4 = row8(fr_ref[pl.ds(b, 1), :]) * (sign * 4.0 / _FTOP)
        heading = row8(wd_ref[pl.ds(b, 1), :])
        dcos = drive4 * jnp.cos(heading)
        dsin = drive4 * jnp.sin(heading)
        for g in range(21):
            rows = slice(8 * g, 8 * g + 8)
            gain = wet * lane_gather(cgx[rows, :], cls)
            gain_ref[rows, lanes] = gain
            base_ref[rows, lanes] = xs_ref[rows, lanes] * (1.0 / SCALE) + gain * total[g]
            r = 8 * (g % 9)
            drive = tab_ref[r : r + 8, :] * dcos + tab_ref[72 + r : 80 + r, :] * dsin
            wind_ref[rows, lanes] = 0.125 * jnp.maximum(fc_ref[rows, :] * drive - 1.0, 0.0)
        return carry

    lax.fori_loop(0, 8, node_block, 0)


def ghost_kernel(
    g0, g1, g2, g3, g4, base_ref, gain_ref, xs_ref, fc_ref, geo_ref, code_ref, tab_ref, adv_ref,
    sums_ref, packed
):
    low = lax.broadcasted_iota(jnp.int32, (8, LANES), 1) < GHOST
    for g in range(11):
        rows = slice(8 * g, 8 * g + 8)
        whole = [(ref[rows, :] * SCALE + 0.5).astype(jnp.int32) for ref in (g0, g1, g2, g3, g4)]
        for q in range(3):
            a = whole[2 * q]
            word = (a << 16) | pltpu.roll(a, 64, 1)
            if q < 2:
                c = whole[2 * q + 1]
                word = jnp.where(low, word, (pltpu.roll(c, 64, 1) << 16) | c)
            packed[rows, LANES * q : LANES * q + LANES] = word

    def node_block(b, carry):
        lanes = pl.ds(pl.multiple_of(b * LANES, LANES), LANES)
        total = [jnp.zeros((8, LANES), jnp.float32) for _ in range(21)]
        for m in range(8):
            full = row8(code_ref[m : m + 1, lanes])
            index = full & 127
            bits = [(full & 128) != 0, (full & 256) != 0]
            wc = row8(geo_ref[0, m : m + 1, lanes])
            ws = row8(geo_ref[1, m : m + 1, lanes])
            for g in range(11):
                word = pick(
                    [packed[8 * g : 8 * g + 8, LANES * s : LANES * s + LANES] for s in range(3)],
                    index,
                    bits,
                )
                for h, value in ((g, lax.shift_right_logical(word, 16)), (g + 11, word & 65535)):
                    if h > 20:
                        continue
                    r = 8 * (h % 9)
                    share = jnp.maximum(
                        tab_ref[r : r + 8, :] * wc + tab_ref[72 + r : 80 + r, :] * ws, 0.0
                    )
                    total[h] = total[h] + share * (
                        value.astype(jnp.float32) - xs_ref[8 * h : 8 * h + 8, lanes]
                    )
        energy = jnp.zeros((8, LANES), jnp.float32)
        moment = jnp.zeros((8, LANES), jnp.float32)
        for g in range(21):
            rows = slice(8 * g, 8 * g + 8)
            adv = base_ref[rows, lanes] + gain_ref[rows, lanes] * total[g]
            adv_ref[rows, lanes] = adv
            freq = fc_ref[rows, :]
            term = freq * adv
            energy = energy + term
            moment = moment + freq * term
        erow = jnp.sum(energy, axis=0, keepdims=True) * _KAPPA
        mrow = jnp.sum(moment, axis=0, keepdims=True) * _KAPPA
        for r in range(8):
            sums_ref[r, pl.ds(b, 1), :] = erow
            sums_ref[r, pl.ds(b + 8, 1), :] = mrow
        return carry

    lax.fori_loop(0, 8, node_block, 0)


def source_kernel(id_ref, sums_ref, adv_ref, wind_ref, fc_ref, out_ref, energy_ref, damp):
    spec = id_ref[1]
    total = sums_ref[0]
    for r in range(1, 8):
        total = total + sums_ref[r]
    energy = total[0:8]
    moment = total[8:16]
    mean = (moment + 4e-8) / (energy + 1e-6)
    scaled = mean / 0.8
    steep = energy * (scaled * scaled) * (scaled * scaled)
    damp[...] = (0.25 * steep) * steep / mean
    mine = lax.broadcasted_iota(jnp.int32, (8, LANES), 0) == spec
    energy_ref[...] = jnp.sum(jnp.where(mine, energy, 0.0), axis=0, keepdims=True)
    for b in range(8):
        lanes = slice(LANES * b, LANES * b + LANES)
        rate = row8(damp[b : b + 1, :])
        for g in range(21):
            n = 8 if g < 20 else 2
            rows = slice(8 * g, 8 * g + 8)
            value = adv_ref[rows, lanes] * jnp.exp(wind_ref[rows, lanes] - rate * fc_ref[rows, :])
            out_ref[8 * g : 8 * g + n, lanes] = value[0:n]


SMEM = pl.BlockSpec(memory_space=pltpu.SMEM)
VMEM = pl.BlockSpec(memory_space=pltpu.VMEM)
F32 = jnp.float32


def shape(*dims, dtype=jnp.float32):
    return jax.ShapeDtypeStruct(dims, dtype)


def cost(flops, size):
    return pl.CostEstimate(flops=flops, bytes_accessed=size, transcendentals=0)


LIMIT = pltpu.CompilerParams(vmem_limit_bytes=32 << 20)


def per_device(
    spectra,
    wet_mask,
    depth_class,
    cg_table,
    neighbour,
    edge_weight,
    edge_angle,
    send_list,
    friction,
    wind_dir,
):
    me = lax.axis_index("space")
    spec = lax.axis_index("spec")
    ids = jnp.stack([me, spec]).astype(jnp.int32)
    wet = wet_mask.reshape(8, LANES)
    table = jnp.asarray(_tables())
    outgoing = pl.pallas_call(
        send_kernel,
        out_shape=shape(5, PACK, LANES),
        in_specs=[SMEM, VMEM, VMEM, VMEM],
        out_specs=VMEM,
        compiler_params=LIMIT,
        name="send_pack",
    )(ids, spectra, wet, send_list[0])
    ghosts = [
        lax.ppermute(outgoing[k], "space", [(i, (i + o) % 32) for i in range(32)])
        for k, o in enumerate(OFFSETS)
    ]
    base, gain, scaled, wind, freq, geo, code = pl.pallas_call(
        local_kernel,
        out_shape=(
            shape(168, 1024),
            shape(168, 1024),
            shape(168, 1024),
            shape(168, 1024),
            shape(168, LANES),
            shape(2, 8, 1024),
            shape(8, 1024, dtype=jnp.int32),
        ),
        in_specs=[SMEM] + [VMEM] * 10,
        out_specs=(VMEM,) * 7,
        scratch_shapes=[
            pltpu.VMEM((PACK, 1024), jnp.int32),
            pltpu.VMEM((168, LANES), F32),
            pltpu.VMEM((2, 8, 1024), F32),
        ],
        compiler_params=LIMIT,
        cost_estimate=cost(20_000_000, 4_000_000),
        name="local_slots",
    )(
        ids,
        spectra,
        wet,
        neighbour,
        edge_weight,
        edge_angle,
        depth_class.reshape(8, LANES),
        cg_table,
        friction.reshape(8, LANES),
        wind_dir.reshape(8, LANES),
        table,
    )
    advected, sums = pl.pallas_call(
        ghost_kernel,
        out_shape=(shape(168, 1024), shape(8, 16, LANES)),
        in_specs=[VMEM] * 12,
        out_specs=(VMEM,) * 2,
        scratch_shapes=[pltpu.VMEM((PACK, 3 * LANES), jnp.int32)],
        compiler_params=LIMIT,
        name="ghost_slots",
    )(*ghosts, base, gain, scaled, freq, geo, code, table)
    parts = lax.all_to_all(sums, "spec", split_axis=0, concat_axis=0, tiled=True)
    result, energy = pl.pallas_call(
        source_kernel,
        out_shape=(shape(162, 1024), shape(1, LANES)),
        in_specs=[SMEM] + [VMEM] * 4,
        out_specs=(VMEM,) * 2,
        scratch_shapes=[pltpu.VMEM((8, LANES), F32)],
        compiler_params=LIMIT,
        name="source",
    )(ids, parts, advected, wind, freq)
    return result, energy.reshape(LANES)


def solution(mesh):
    placed = (
        P("spec", "space"),
        P("space"),
        P("space"),
        P(),
        P(None, "space"),
        P(None, "space"),
        P(None, "space"),
        P("space", None, None),
        P("space"),
        P("space"),
    )
    return jax.shard_map(
        per_device,
        mesh=mesh,
        in_specs=placed,
        out_specs=(P("spec", "space"), P(("space", "spec"))),
        check_vma=False,
    )
```

time: 214 us -> 45.7 us (0.21); the launches traced: 212 us -> 45.4 us
  other arithmetic: 112 us -> 0.08 us
  local copies, waits for them, and re-layouts: 62.7 us -> 2.52 us
  Pallas kernels: 0 us -> 15.7 us
  blocking collectives: 15.6 us -> 10.7 us
  matrix products: 2.4 us -> 0 us
    gather x69 -> x0, other arithmetic: 75.6 us -> none  [the longest x31 24.8 us: per_device(): dir_cosine[full_dir]]
    gather x15 -> x0, local copies, waits for them, and re-layouts: 56.1 us -> none  [the longest x2 39.8 us: per_device(): gathered_all = jnp.take(extended, neighbour.reshape(-1), axis=1)]
    div x2 -> x0, other arithmetic: 18 us -> none  [the longest x1 18 us: point_source(): relative = freq_col / top_freq]
    all_to_all x2 -> x0, starting transfers between devices: 17.4 us -> none  [the longest x1 12.2 us: per_device(): lax.all_to_all(outgoing, 'space', split_axis=1, concat_axis=1, tiled=True)]
    pallas_call x0 -> x4, Pallas kernels: none -> 15.7 us  [the longest x1 8.1 us: per_device(): pl.pallas_call(local_kernel, out_shape=(shape(168, 1024), shape(168, 1024...]
    ppermute x0 -> x5, starting transfers between devices: none -> 15.6 us  [per_device(): lax.ppermute(outgoing[k], 'space', [(i, (i + o) % 32) for i in range(32)])]
    all_to_all x1 -> x0, other arithmetic: 5.48 us -> none  [per_device(): lax.all_to_all(updated.reshape(comp_count * spec_count, 1, point_count),...]
    all_to_all x1, blocking collectives: 15.6 us -> 10.7 us  [per_device(): lax.all_to_all(sums, 'spec', split_axis=0, concat_axis=0, tiled=True)]
  transfers between devices with their start and end apart: 2 -> 5, of which waited for: 0 -> 0; matrix products, arithmetic and copies ran while one was open for 50% -> 0% of each run, Pallas kernels for 0% -> 18%
where the time goes in v1:
time: 45.7 us; the launch traced here: 45.4 us
  Pallas kernels  15.7 us (34%)
  starting transfers between devices  15.6 us (34%)
  blocking collectives  10.7 us (23%)
  local copies, waits for them, and re-layouts  2.52 us (6%)
  between operations  0.8 us (2%)
    ppermute x5, starting transfers between devices, per_device(): lax.ppermute(outgoing[k], 'space', [(i, (i + o) % 32) for i in range(32)])  15.6 us
    all_to_all x1, blocking collectives, per_device(): lax.all_to_all(sums, 'spec', split_axis=0, concat_axis=0, tiled=True)  10.7 us
    pallas_call x1, Pallas kernels, per_device(): pl.pallas_call(local_kernel, out_shape=(shape(168, 1024), shape(168, 1024...  8.1 us
    pallas_call x1, Pallas kernels, per_device(): pl.pallas_call(ghost_kernel, out_shape=(shape(168, 1024), shape(8, 16, LA...  3.54 us
    unnamed x25, local copies, waits for them, and re-layouts  2.5 us
    pallas_call x1, Pallas kernels, per_device(): pl.pallas_call(send_kernel, out_shape=shape(5, PACK, LANES), in_specs=[SM...  2.49 us
    pallas_call x1, Pallas kernels, per_device(): pl.pallas_call(source_kernel, out_shape=(shape(162, 1024), shape(1, LANES...  1.58 us
  transfers between devices with their start and end apart: 5, of which 0 were waited for; matrix products, arithmetic and copies ran while one was open for 0% of the time, Pallas kernels for 18%

profile of v1, /device:TPU:1, one launch (start us, length us, event | category | flops | bytes accessed | tf_op | source)
XLA Modules:
  0.0 45.4 jit_solution(15948615291430897550)
XLA Ops:
  0.6 0.0 copy-start.6
  0.6 0.0 copy-start.7
  0.7 0.1 pad_add_fusion.me_ref.id_ref
  0.7 0.6 %copy-done.6 = s32[1,32,64]{2,1,0:T(8,128)S(1)} copy-done((s32[1,32,64]{2,1,0:T(8,128)S(1)}, s32[1,32,64]{2,1,0:T(8,128)}, u32[]{:S(2)}) %copy-start.6) | copy-done | bytes 8216
  1.3 0.0 copy-done.7
  1.4 1.1 %copy-done = f32[162,1024]{1,0:T(8,128)S(1)} copy-done((f32[162,1024]{1,0:T(8,128)S(1)}, f32[162,1024]{1,0:T(8,128)}, u32[]{:S(2)}) %copy-start) | copy-done | bytes 663576
  2.5 2.5 %send_pack.1 = f32[5,88,128]{2,1,0:T(8,128)S(1)} custom-call(s32[2]{0:T(128)S(1)} %pad_add_fusion.me_ref.id_ref, f32[162,1024]{1,0:T(8,128)S(1)} %copy-done, s32[8,128]{1,0:T(8,128)S(1)} %bitcast.19, s32[32,64]{1,0:T(8,128)S(1)} %bitcast.18), custom_call_target="tpu_custom_call" | custom-call | tf_op jit(solution)/shard_map/send_pack/pallas_call | solution.py:322
  4.9 0.0 copy-start.11
  5.0 0.0 copy-start.2
  5.0 0.0 copy-start.4
  5.0 0.0 copy-start.5
  5.0 0.0 copy-start.3
  5.0 3.8 %collective-permute-start.4 = (f32[88,128]{1,0:T(8,128)S(1)}, f32[88,128]{1,0:T(8,128)S(1)}, u32[]{:S(2)}, u32[]{:S(2)}) collective-permute-start(f32[88,128]{1,0:T(8,128)S(1)} %get-tuple-element.24), channel_id=1, source_target_pairs={{0,128},{8,136},{16,144},{24,152},{32,160},{40,168},{48,176},{56,1... | collective-permute-start | bytes 135176 | tf_op jit(solution)/shard_map/ppermute | solution.py:331
  8.9 6.5 %collective-permute-start.3 = (f32[88,128]{1,0:T(8,128)S(1)}, f32[88,128]{1,0:T(8,128)S(1)}, u32[]{:S(2)}, u32[]{:S(2)}) collective-permute-start(f32[88,128]{1,0:T(8,128)S(1)} %get-tuple-element.25), channel_id=1, source_target_pairs={{0,240},{8,248},{16,0},{24,8},{32,16},{40,24},{48,32},{56,40},{64,... | collective-permute-start | bytes 135176 | tf_op jit(solution)/shard_map/ppermute | solution.py:331
  15.4 0.0 collective-permute-start.2
  15.4 5.2 %collective-permute-start.1 = (f32[88,128]{1,0:T(8,128)S(1)}, f32[88,128]{1,0:T(8,128)S(1)}, u32[]{:S(2)}, u32[]{:S(2)}) collective-permute-start(f32[88,128]{1,0:T(8,128)S(1)} %get-tuple-element.27), channel_id=1, source_target_pairs={{0,248},{8,0},{16,8},{24,16},{32,24},{40,32},{48,40},{56,48},{64,5... | collective-permute-start | bytes 135176 | tf_op jit(solution)/shard_map/ppermute | solution.py:331
  20.6 0.0 collective-permute-start
  20.6 0.0 copy-done.11
  20.6 0.1 copy.13.cg_ref
  20.7 0.0 copy-done.1
  20.8 0.6 %copy-done.9 = f32[1024]{0:T(1024)S(1)} copy-done((f32[1024]{0:T(1024)S(1)}, f32[1024]{0:T(1024)}, u32[]{:S(2)}) %copy-start.9) | copy-done | bytes 4120
  21.3 0.0 copy-done.10
  21.3 0.1 copy-done.8
  21.4 8.1 %local_slots.1 = (f32[168,1024]{1,0:T(8,128)S(1)}, f32[168,1024]{1,0:T(8,128)S(1)}, f32[168,1024]{1,0:T(8,128)S(1)}, f32[168,1024]{1,0:T(8,128)S(1)}, f32[168,12...) custom-call(s32[2]{0:T(128)S(1)} %pad_add_fusion.me_ref.id_ref, f32[162,1024]{1,0:T(8,128)S(1)} %copy-done.1, ...), custom_call_target="tpu_custom_call" | custom-call | flops 20000000 | bytes 4000000 | tf_op jit(solution)/shard_map/local_slots/pallas_call | solution.py:334
  29.5 0.0 collective-permute-done.4.g4
  29.5 0.0 collective-permute-done.3.g3
  29.5 0.0 collective-permute-done.2.g2
  29.5 0.0 collective-permute-done.1.g1
  29.6 0.0 collective-permute-done.g0
  29.6 3.5 %ghost_slots.1 = (f32[168,1024]{1,0:T(8,128)S(1)}, f32[8,16,128]{2,1,0:T(8,128)S(1)}) custom-call(f32[88,128]{1,0:T(8,128)S(1)} %collective-permute-done.g0, f32[88,128]{1,0:T(8,128)S(1)} %collective-permute-done.1.g1, f32[88,128]{1,0:T(8,128)S(1)} %collective-permute-done.2.g2, f32[88,128]{1,0:T(8,128)S(1)} %collective-permute-done.3.g3, ...), custom_call_target="tpu_custom_call" | custom-call | tf_op jit(solution)/shard_map/ghost_slots/pallas_call | solution.py:368
  33.1 10.7 %all_to_all.5.sums_ref = f32[8,16,128]{2,1,0:T(8,128)S(1)} all-to-all(f32[8,16,128]{2,1,0:T(8,128)S(1)} %get-tuple-element.19), channel_id=1, replica_groups=mesh['space'=32,'spec'=8] {'spec'}, dimensions={0} | all-to-all | bytes 131072 | tf_op jit(solution)/shard_map/all_to_all | solution.py:377
  43.8 1.6 %source.1 = (f32[162,1024]{1,0:T(8,128)}, f32[1,128]{1,0:T(1,128)}) custom-call(s32[2]{0:T(128)S(1)} %pad_add_fusion.me_ref.id_ref, f32[8,16,128]{2,1,0:T(8,128)S(1)} %all_to_all.5.sums_ref, f32[168,1024]{1,0:T(8,128)S(1)} %get-tuple-element.20.adv_ref, f32[168,1024]{1,0:T(8,128)S(1)} %get-tuple-element.21.wind_ref, f32[168,128]{1,0:T(8,128)S(1)} %get-tuple-element.16.fc_ref), custom_call_target="tpu_custom_call" | custom-call | tf_op jit(solution)/shard_map/source/pallas_call | solution.py:378
  (10 shorter events, 0.0 us)
Async XLA Ops:
  0.6 0.7 %copy-start.6 = (s32[1,32,64]{2,1,0:T(8,128)S(1)}, s32[1,32,64]{2,1,0:T(8,128)}, u32[]{:S(2)}) copy-start(s32[1,32,64]{2,1,0:T(8,128)} %param.18) | copy-start | bytes 24580
  0.6 0.7 %copy-start.7 = (s32[1024]{0:T(1024)S(1)}, s32[1024]{0:T(1024)}, u32[]{:S(2)}) copy-start(s32[1024]{0:T(1024)} %param.12) | copy-start | bytes 12292
  1.4 1.1 %copy-start = (f32[162,1024]{1,0:T(8,128)S(1)}, f32[162,1024]{1,0:T(8,128)}, u32[]{:S(2)}) copy-start(f32[162,1024]{1,0:T(8,128)} %x_ref.3) | copy-start | bytes 1990660
  2.5 18.3 %copy-start.1 = (f32[162,1024]{1,0:T(8,128)S(1)}, f32[162,1024]{1,0:T(8,128)}, u32[]{:S(2)}) copy-start(f32[162,1024]{1,0:T(8,128)} %x_ref.3) | copy-start | bytes 1990660
  4.9 15.7 %copy-start.11 = (f32[36,32]{0,1:T(8,128)S(1)}, f32[36,32]{0,1:T(8,128)}, u32[]{:S(2)}) copy-start(f32[36,32]{0,1:T(8,128)} %param.14) | copy-start | bytes 13828
  5.0 15.8 %copy-start.2 = (f32[184,128]{1,0:T(8,128)S(1)}, f32[184,128]{1,0:T(8,128)}, u32[]{:S(2)}) copy-start(f32[184,128]{1,0:T(8,128)} %constant.11.clone.tab_ref) | copy-start | bytes 282628
  5.0 15.8 %copy-start.4 = (f32[8,1024]{1,0:T(8,128)S(1)}, f32[8,1024]{1,0:T(8,128)}, u32[]{:S(2)}) copy-start(f32[8,1024]{1,0:T(8,128)} %ew_ref.1) | copy-start | bytes 98308
  5.0 15.8 %copy-start.5 = (f32[8,1024]{1,0:T(8,128)S(1)}, f32[8,1024]{1,0:T(8,128)}, u32[]{:S(2)}) copy-start(f32[8,1024]{1,0:T(8,128)} %ea_ref.1) | copy-start | bytes 98308
  5.0 15.7 %copy-start.3 = (s32[8,1024]{1,0:T(8,128)S(1)}, s32[8,1024]{1,0:T(8,128)}, u32[]{:S(2)}) copy-start(s32[8,1024]{1,0:T(8,128)} %nb_ref.1) | copy-start | bytes 98308
  5.0 24.5 %collective-permute-start.4 = (f32[88,128]{1,0:T(8,128)S(1)}, f32[88,128]{1,0:T(8,128)S(1)}, u32[]{:S(2)}, u32[]{:S(2)}) collective-permute-start(f32[88,128]{1,0:T(8,128)S(1)} %get-tuple-element.24), channel_id=1, source_target_pairs={{0,128},{8,136},{16,144},{24,152},{32,160},{40,168},{48,176},{56,1... | collective-permute-start | bytes 135176 | tf_op jit(solution)/shard_map/ppermute | solution.py:331
  8.9 20.7 %collective-permute-start.3 = (f32[88,128]{1,0:T(8,128)S(1)}, f32[88,128]{1,0:T(8,128)S(1)}, u32[]{:S(2)}, u32[]{:S(2)}) collective-permute-start(f32[88,128]{1,0:T(8,128)S(1)} %get-tuple-element.25), channel_id=1, source_target_pairs={{0,240},{8,248},{16,0},{24,8},{32,16},{40,24},{48,32},{56,40},{64,... | collective-permute-start | bytes 135176 | tf_op jit(solution)/shard_map/ppermute | solution.py:331
  15.4 14.2 %collective-permute-start.2 = (f32[88,128]{1,0:T(8,128)S(1)}, f32[88,128]{1,0:T(8,128)S(1)}, u32[]{:S(2)}, u32[]{:S(2)}) collective-permute-start(f32[88,128]{1,0:T(8,128)S(1)} %get-tuple-element.26), channel_id=1, source_target_pairs={{0,16},{8,24},{16,32},{24,40},{32,48},{40,56},{48,64},{56,72},{64,... | collective-permute-start | bytes 135176 | tf_op jit(solution)/shard_map/ppermute | solution.py:331
  15.4 14.2 %collective-permute-start.1 = (f32[88,128]{1,0:T(8,128)S(1)}, f32[88,128]{1,0:T(8,128)S(1)}, u32[]{:S(2)}, u32[]{:S(2)}) collective-permute-start(f32[88,128]{1,0:T(8,128)S(1)} %get-tuple-element.27), channel_id=1, source_target_pairs={{0,248},{8,0},{16,8},{24,16},{32,24},{40,32},{48,40},{56,48},{64,5... | collective-permute-start | bytes 135176 | tf_op jit(solution)/shard_map/ppermute | solution.py:331
  20.6 8.9 %collective-permute-start = (f32[88,128]{1,0:T(8,128)S(1)}, f32[88,128]{1,0:T(8,128)S(1)}, u32[]{:S(2)}, u32[]{:S(2)}) collective-permute-start(f32[88,128]{1,0:T(8,128)S(1)} %get-tuple-element.28), channel_id=1, source_target_pairs={{0,8},{8,16},{16,24},{24,32},{32,40},{40,48},{48,56},{56,64},{64,7... | collective-permute-start | bytes 135176 | tf_op jit(solution)/shard_map/ppermute | solution.py:331
  20.6 0.7 %copy-start.9 = (f32[1024]{0:T(1024)S(1)}, f32[1024]{0:T(1024)}, u32[]{:S(2)}) copy-start(f32[1024]{0:T(1024)} %param.19) | copy-start | bytes 12292
  20.6 0.7 %copy-start.10 = (f32[1024]{0:T(1024)S(1)}, f32[1024]{0:T(1024)}, u32[]{:S(2)}) copy-start(f32[1024]{0:T(1024)} %param.20) | copy-start | bytes 12292
  20.7 0.7 %copy-start.8 = (s32[1024]{0:T(1024)S(1)}, s32[1024]{0:T(1024)}, u32[]{:S(2)}) copy-start(s32[1024]{0:T(1024)} %param.13) | copy-start | bytes 12292

commit v2 on v1

v2 whole, which is shorter than its diff:
```python
import math

import numpy as np
import jax
import jax.numpy as jnp
from jax import lax
from jax.experimental import pallas as pl
from jax.experimental.pallas import tpu as pltpu
from jax.sharding import PartitionSpec as P

NDIR = 36
NFREQ = 36
GHOST = 64
LANES = 128
PACK = 88
OFFSETS = (1, 31, 2, 30, 16)
SCALE = 32767.5

_F = 0.04 * np.exp(np.arange(NFREQ) * math.log(1.1))
_KAPPA = float(0.1 / (NDIR * np.sum(0.1 * _F)))
_FTOP = float(_F[-1])


def _tables():
    angle = 2.0 * np.pi * (np.arange(72) % NDIR) / NDIR
    cosine = np.repeat(np.cos(angle)[:, None], LANES, 1)
    sine = np.repeat(np.sin(angle)[:, None], LANES, 1)
    freq = np.zeros((40, LANES))
    freq[:NFREQ] = _F[:, None]
    return np.concatenate([cosine, sine, freq]).astype(np.float32)


def lane_gather(values, index):
    return jnp.take_along_axis(values, index, axis=1, mode="promise_in_bounds")


def pick(blocks, index, bits):
    level = [lane_gather(block, index) for block in blocks]
    for bit in bits:
        level = [
            jnp.where(bit, level[i + 1], level[i]) if i + 1 < len(level) else level[i]
            for i in range(0, len(level), 2)
        ]
    return level[0]


def row8(row):
    return jnp.broadcast_to(row, (8, LANES))


def turn(angle):
    h = 0.5 * angle
    t = h * h
    s = h * (
        1.0
        + t
        * (
            -1.6666666666e-1
            + t * (8.3333331e-3 + t * (-1.98412e-4 + t * (2.75567e-6 - t * 2.4700e-8)))
        )
    )
    c = 1.0 + t * (
        -0.5
        + t * (4.16666664e-2 + t * (-1.3888883e-3 + t * (2.480065e-5 + t * (-2.75358e-7 + t * 2.065e-9))))
    )
    return 1.0 - 2.0 * s * s, 2.0 * s * c


CHUNKS = ((0, 6), (6, 11))


def send_kernel(
    x_hbm, plan_ref, o0, o1, o2, o3, o4, masked_ref, packed_ref, x_ref, code_ref,
    words_ref, sem
):
    outs = (o0, o1, o2, o3, o4)
    copies = []
    for i, (first, last) in enumerate(CHUNKS):
        for j, base in enumerate((0, PACK)):
            rows = pl.ds(base + 8 * first, min(8 * last + base, 162) - base - 8 * first)
            copies.append(
                pltpu.make_async_copy(x_hbm.at[rows, :], x_ref.at[rows, :], sem.at[2 * i + j])
            )
    for copy in copies:
        copy.start()
    me = lax.axis_index("space")
    lane = lax.broadcasted_iota(jnp.int32, (8, LANES), 1)
    low = lane < GHOST
    rows = [plan_ref[pl.ds(8 + ((me + o) & 31), 1), 0:GHOST] for o in OFFSETS]
    for q, (a, b) in enumerate(((0, 1), (2, 3), (4, 4))):
        code_ref[q] = row8(jnp.concatenate([rows[a], rows[b]], axis=1))
    wet = [row8(plan_ref[b : b + 1, :].astype(jnp.float32)) for b in range(8)]

    def load(g, b):
        lanes = slice(LANES * b, LANES * b + LANES)
        if g < 20:
            value = x_ref[8 * g : 8 * g + 8, lanes] * wet[b]
        else:
            zero = jnp.zeros((6, LANES), jnp.float32)
            value = jnp.concatenate([x_ref[160:162, lanes], zero], axis=0) * wet[b]
        masked_ref[8 * g : 8 * g + 8, lanes] = value
        return (value * SCALE + 0.5).astype(jnp.int32)

    for i, (first, last) in enumerate(CHUNKS):
        copies[2 * i].wait()
        copies[2 * i + 1].wait()
        for g in range(first, last):
            for b in range(8):
                word = load(g, b) << 16
                if g < 10:
                    word = word | load(g + 11, b)
                packed_ref[8 * g : 8 * g + 8, LANES * b : LANES * b + LANES] = word

    def gather(q, carry):
        full = code_ref[q]
        index = full & 127
        bits = [(full & (128 << i)) != 0 for i in range(3)]
        for g in range(11):
            rows = slice(8 * g, 8 * g + 8)
            words_ref[q, rows, :] = pick(
                [packed_ref[rows, LANES * b : LANES * b + LANES] for b in range(8)], index, bits
            )
        return carry

    lax.fori_loop(0, 3, gather, 0)
    for q in range(3):
        for g in range(11):
            rows = slice(8 * g, 8 * g + 8)
            word = words_ref[q, rows, :]
            top = lax.shift_right_logical(word, 16).astype(jnp.float32)
            bottom = (word & 65535).astype(jnp.float32)
            if q < 2:
                outs[2 * q][rows, :] = jnp.where(low, top, pltpu.roll(bottom, 64, 1))
                outs[2 * q + 1][rows, :] = jnp.where(low, pltpu.roll(top, 64, 1), bottom)
            else:
                outs[4][rows, :] = jnp.where(low, top, bottom)


def slots(packed, blocks, code, geo, tab_ref, lanes, bit_count):
    total = [None] * 21
    shares = [None] * 9
    for m in range(8):
        full = row8(code[m : m + 1, lanes])
        index = full & 127
        bits = [(full & (128 << i)) != 0 for i in range(bit_count)]
        wc = row8(geo[0, m : m + 1, lanes])
        ws = row8(geo[1, m : m + 1, lanes])
        share = [
            jnp.maximum(
                tab_ref[8 * r : 8 * r + 8, :] * wc + tab_ref[72 + 8 * r : 80 + 8 * r, :] * ws, 0.0
            )
            for r in range(9)
        ]
        shares = [s if t is None else t + s for t, s in zip(shares, share)]
        for g in range(11):
            word = pick(
                [packed[8 * g : 8 * g + 8, LANES * s : LANES * s + LANES] for s in range(blocks)],
                index,
                bits,
            )
            for h, value in ((g, lax.shift_right_logical(word, 16)), (g + 11, word & 65535)):
                if h < 21:
                    term = share[h % 9] * value.astype(jnp.float32)
                    total[h] = term if total[h] is None else total[h] + term
    return total, shares


def local_kernel(
    x_ref,
    packed,
    wet_ref,
    nb_ref,
    ew_ref,
    ea_ref,
    dc_ref,
    cg_ref,
    fr_ref,
    wd_ref,
    tab_ref,
    base_ref,
    gain_ref,
    wind_ref,
    fc_ref,
    geo_ref,
    code_ref,
    cgx,
    wloc,
    drive_ref,
):
    me = lax.axis_index("space")
    spec = lax.axis_index("spec")
    par = spec & 1
    first_freq = (9 * spec) >> 1
    sign = (1 - 2 * par).astype(jnp.float32)
    entry = nb_ref[...]
    ghost = entry >= 1024
    weight = ew_ref[...] * sign
    cosine, sine = turn(ea_ref[...])
    wc = weight * cosine
    ws = weight * sine
    wloc[0] = jnp.where(ghost, 0.0, wc)
    wloc[1] = jnp.where(ghost, 0.0, ws)
    geo_ref[0] = jnp.where(ghost, wc, 0.0)
    geo_ref[1] = jnp.where(ghost, ws, 0.0)
    peer = (entry - 1024) >> 6
    off = (me - peer) & 31
    half = (off == 31) | (off == 30)
    block = jnp.where(off == 16, 2, jnp.where((off == 2) | (off == 30), 1, 0))
    code_ref[...] = (entry & 63) + jnp.where(half, 64, 0) + 128 * block
    drive4 = fr_ref[...] * (sign * 4.0 / _FTOP)
    cosine, sine = turn(wd_ref[...])
    drive_ref[0] = drive4 * cosine
    drive_ref[1] = drive4 * sine
    cgpad = [None] * 5
    fpad = [None] * 5
    for j in range(5):
        line = cg_ref[pl.ds(first_freq + j, 1), :]
        cgpad[j] = row8(jnp.concatenate([line, line, line, line], axis=1))
        fpad[j] = row8(tab_ref[pl.ds(144 + first_freq + j, 1), :])
    for g in range(21):
        comp = lax.broadcasted_iota(jnp.int32, (8, LANES), 0) + 8 * g + 18 * par
        cv, fv = cgpad[0], fpad[0]
        for j in range(1, 5):
            if 8 * g + 7 + 18 >= 36 * j:
                later = comp >= 36 * j
                cv = jnp.where(later, cgpad[j], cv)
                fv = jnp.where(later, fpad[j], fv)
        cgx[8 * g : 8 * g + 8, :] = cv
        fc_ref[8 * g : 8 * g + 8, :] = fv

    def node_block(b, carry):
        lanes = pl.ds(pl.multiple_of(b * LANES, LANES), LANES)
        wet = row8(wet_ref[pl.ds(b, 1), :].astype(jnp.float32))
        cls = row8(dc_ref[pl.ds(b, 1), :])
        total, shares = slots(packed, 8, nb_ref, wloc, tab_ref, lanes, 3)
        dcos = row8(drive_ref[0, pl.ds(b, 1), :])
        dsin = row8(drive_ref[1, pl.ds(b, 1), :])
        for g in range(21):
            rows = slice(8 * g, 8 * g + 8)
            gain = wet * lane_gather(cgx[rows, :], cls)
            gain_ref[rows, lanes] = gain
            x = x_ref[rows, lanes]
            base_ref[rows, lanes] = x + gain * (total[g] * (1.0 / SCALE) - x * shares[g % 9])
            r = 8 * (g % 9)
            drive = tab_ref[r : r + 8, :] * dcos + tab_ref[72 + r : 80 + r, :] * dsin
            wind_ref[rows, lanes] = 0.125 * jnp.maximum(fc_ref[rows, :] * drive - 1.0, 0.0)
        return carry

    lax.fori_loop(0, 8, node_block, 0, unroll=2)


def ghost_kernel(
    g0, g1, g2, g3, g4, x_ref, base_ref, gain_ref, fc_ref, geo_ref, code_ref, tab_ref, adv_ref,
    sums_ref, packed
):
    low = lax.broadcasted_iota(jnp.int32, (8, LANES), 1) < GHOST
    for g in range(11):
        rows = slice(8 * g, 8 * g + 8)
        whole = [ref[rows, :].astype(jnp.int32) for ref in (g0, g1, g2, g3, g4)]
        for q in range(3):
            a = whole[2 * q]
            word = (a << 16) | pltpu.roll(a, 64, 1)
            if q < 2:
                c = whole[2 * q + 1]
                word = jnp.where(low, word, (pltpu.roll(c, 64, 1) << 16) | c)
            packed[rows, LANES * q : LANES * q + LANES] = word

    def node_block(b, carry):
        lanes = pl.ds(pl.multiple_of(b * LANES, LANES), LANES)
        total, shares = slots(packed, 3, code_ref, geo_ref, tab_ref, lanes, 2)
        energy = jnp.zeros((8, LANES), jnp.float32)
        moment = jnp.zeros((8, LANES), jnp.float32)
        for g in range(21):
            rows = slice(8 * g, 8 * g + 8)
            inflow = total[g] * (1.0 / SCALE) - x_ref[rows, lanes] * shares[g % 9]
            adv = base_ref[rows, lanes] + gain_ref[rows, lanes] * inflow
            adv_ref[rows, lanes] = adv
            freq = fc_ref[rows, :]
            term = freq * adv
            energy = energy + term
            moment = moment + freq * term
        erow = jnp.sum(energy, axis=0, keepdims=True) * _KAPPA
        mrow = jnp.sum(moment, axis=0, keepdims=True) * _KAPPA
        for r in range(8):
            sums_ref[r, pl.ds(b, 1), :] = erow
            sums_ref[r, pl.ds(b + 8, 1), :] = mrow
        return carry

    lax.fori_loop(0, 8, node_block, 0, unroll=4)


OUT_ROWS = ((0, 5), (5, 10), (10, 15), (15, 21))


def source_kernel(sums_ref, adv_ref, wind_ref, fc_ref, out_hbm, energy_ref, damp, out_ref, sem):
    spec = lax.axis_index("spec")
    total = sums_ref[0]
    for r in range(1, 8):
        total = total + sums_ref[r]
    energy = total[0:8]
    moment = total[8:16]
    mean = (moment + 4e-8) / (energy + 1e-6)
    scaled = mean / 0.8
    steep = energy * (scaled * scaled) * (scaled * scaled)
    damp[...] = (0.25 * steep) * steep / mean
    mine = lax.broadcasted_iota(jnp.int32, (8, LANES), 0) == spec
    energy_ref[...] = jnp.sum(jnp.where(mine, energy, 0.0), axis=0, keepdims=True)
    rate = [row8(damp[b : b + 1, :]) for b in range(8)]
    copies = []
    for i, (first, last) in enumerate(OUT_ROWS):
        for g in range(first, last):
            n = 8 if g < 20 else 2
            rows = slice(8 * g, 8 * g + 8)
            freq = fc_ref[rows, :]
            for b in range(8):
                lanes = slice(LANES * b, LANES * b + LANES)
                value = adv_ref[rows, lanes] * jnp.exp(wind_ref[rows, lanes] - rate[b] * freq)
                out_ref[8 * g : 8 * g + n, lanes] = value[0:n]
        rows = pl.ds(8 * first, min(8 * last, 162) - 8 * first)
        copies.append(
            pltpu.make_async_copy(out_ref.at[rows, :], out_hbm.at[rows, :], sem.at[i])
        )
        copies[i].start()
    for copy in copies:
        copy.wait()


VMEM = pl.BlockSpec(memory_space=pltpu.VMEM)
ANY = pl.BlockSpec(memory_space=pl.ANY)
F32 = jnp.float32
I32 = jnp.int32


def shape(*dims, dtype=jnp.float32):
    return jax.ShapeDtypeStruct(dims, dtype)


def cost(flops, size):
    return pl.CostEstimate(flops=flops, bytes_accessed=size, transcendentals=0)


LIMIT = pltpu.CompilerParams(vmem_limit_bytes=24 << 20)


def per_device(
    spectra,
    wet_mask,
    depth_class,
    cg_table,
    neighbour,
    edge_weight,
    edge_angle,
    send_list,
    friction,
    wind_dir,
):
    wet = wet_mask.reshape(8, LANES)
    table = jnp.asarray(_tables())
    plan = jnp.concatenate([wet, jnp.pad(send_list[0], ((0, 0), (0, LANES - GHOST)))])
    *outgoing, masked, packed = pl.pallas_call(
        send_kernel,
        out_shape=(shape(PACK, LANES),) * 5 + (shape(168, 1024), shape(PACK, 1024, dtype=I32)),
        in_specs=[ANY, VMEM],
        out_specs=(VMEM,) * 7,
        scratch_shapes=[
            pltpu.VMEM((162, 1024), F32),
            pltpu.VMEM((3, 8, LANES), I32),
            pltpu.VMEM((3, PACK, LANES), I32),
            pltpu.SemaphoreType.DMA((4,)),
        ],
        compiler_params=pltpu.CompilerParams(vmem_limit_bytes=53600 << 10),
        name="send_pack",
    )(spectra, plan)
    ghosts = [
        lax.ppermute(outgoing[k], "space", [(i, (i + o) % 32) for i in range(32)])
        for k, o in enumerate(OFFSETS)
    ]
    base, gain, wind, freq, geo, code = pl.pallas_call(
        local_kernel,
        out_shape=(
            shape(168, 1024),
            shape(168, 1024),
            shape(168, 1024),
            shape(168, LANES),
            shape(2, 8, 1024),
            shape(8, 1024, dtype=I32),
        ),
        in_specs=[VMEM] * 11,
        out_specs=(VMEM,) * 6,
        scratch_shapes=[
            pltpu.VMEM((168, LANES), F32),
            pltpu.VMEM((2, 8, 1024), F32),
            pltpu.VMEM((2, 8, LANES), F32),
        ],
        compiler_params=LIMIT,
        cost_estimate=cost(20_000_000, 4_000_000),
        name="local_slots",
    )(
        masked,
        packed,
        wet,
        neighbour,
        edge_weight,
        edge_angle,
        depth_class.reshape(8, LANES),
        cg_table,
        friction.reshape(8, LANES),
        wind_dir.reshape(8, LANES),
        table,
    )
    advected, sums = pl.pallas_call(
        ghost_kernel,
        out_shape=(shape(168, 1024), shape(8, 16, LANES)),
        in_specs=[VMEM] * 12,
        out_specs=(VMEM,) * 2,
        scratch_shapes=[pltpu.VMEM((PACK, 3 * LANES), I32)],
        compiler_params=LIMIT,
        name="ghost_slots",
    )(*ghosts, masked, base, gain, freq, geo, code, table)
    parts = lax.all_to_all(sums, "spec", split_axis=0, concat_axis=0, tiled=True)
    result, energy = pl.pallas_call(
        source_kernel,
        out_shape=(shape(162, 1024), shape(1, LANES)),
        in_specs=[VMEM] * 4,
        out_specs=(ANY, VMEM),
        scratch_shapes=[
            pltpu.VMEM((8, LANES), F32),
            pltpu.VMEM((162, 1024), F32),
            pltpu.SemaphoreType.DMA((4,)),
        ],
        compiler_params=LIMIT,
        name="source",
    )(parts, advected, wind, freq)
    return result, energy.reshape(LANES)


def solution(mesh):
    placed = (
        P("spec", "space"),
        P("space"),
        P("space"),
        P(),
        P(None, "space"),
        P(None, "space"),
        P(None, "space"),
        P("space", None, None),
        P("space"),
        P("space"),
    )
    return jax.shard_map(
        per_device,
        mesh=mesh,
        in_specs=placed,
        out_specs=(P("spec", "space"), P(("space", "spec"))),
        check_vma=False,
    )
```

time: 45.7 us -> 41.3 us (0.904)
  Pallas kernels: 15.7 us -> 13.6 us
  local copies, waits for them, and re-layouts: 2.52 us -> 0.78 us
  starting transfers between devices: 15.6 us -> 14.7 us
  other arithmetic: 0.08 us -> 0.73 us
    unnamed x25 -> x19, local copies, waits for them, and re-layouts: 2.5 us -> 0.78 us
    ppermute x5, starting transfers between devices: 15.6 us -> 14.7 us  [per_device(): lax.ppermute(outgoing[k], 'space', [(i, (i + o) % 32) for i in range(32)])]
    pallas_call x1, Pallas kernels: 8.1 us -> 7.26 us  [per_device(): pl.pallas_call(local_kernel, out_shape=(shape(168, 1024), shape(168, 1024...]
    concatenate x0 -> x1, other arithmetic: none -> 0.73 us  [per_device(): jnp.concatenate([wet, jnp.pad(send_list[0], ((0, 0), (0, LANES - GHOST)))])]
    pallas_call x1, Pallas kernels: 3.54 us -> 2.93 us  [per_device(): pl.pallas_call(ghost_kernel, out_shape=(shape(168, 1024), shape(8, 16, LA...]
    pallas_call x1, Pallas kernels: 2.49 us -> 1.94 us  [per_device(): pl.pallas_call(send_kernel, out_shape=(shape(PACK, LANES),) * 5 + (shape(...]
where the time goes in v2:
time: 41.3 us; the launch traced here: 41 us
  starting transfers between devices  14.7 us (36%)
  Pallas kernels  13.6 us (33%)
  blocking collectives  10.5 us (25%)
  local copies, waits for them, and re-layouts  0.78 us (2%)
  between operations  0.76 us (2%)
  other arithmetic  0.73 us (2%)
    ppermute x5, starting transfers between devices, per_device(): lax.ppermute(outgoing[k], 'space', [(i, (i + o) % 32) for i in range(32)])  14.7 us
    all_to_all x1, blocking collectives, per_device(): lax.all_to_all(sums, 'spec', split_axis=0, concat_axis=0, tiled=True)  10.5 us
    pallas_call x1, Pallas kernels, per_device(): pl.pallas_call(local_kernel, out_shape=(shape(168, 1024), shape(168, 1024...  7.26 us
    pallas_call x1, Pallas kernels, per_device(): pl.pallas_call(ghost_kernel, out_shape=(shape(168, 1024), shape(8, 16, LA...  2.93 us
    pallas_call x1, Pallas kernels, per_device(): pl.pallas_call(send_kernel, out_shape=(shape(PACK, LANES),) * 5 + (shape(...  1.94 us
    pallas_call x1, Pallas kernels, per_device(): pl.pallas_call(source_kernel, out_shape=(shape(162, 1024), shape(1, LANES...  1.45 us
  transfers between devices with their start and end apart: 5, of which 0 were waited for; matrix products, arithmetic and copies ran while one was open for 0% of the time, Pallas kernels for 18%

profile of v2, /device:TPU:1, one launch (start us, length us, event | category | flops | bytes accessed | tf_op | source)
XLA Modules:
  0.0 41.0 jit_solution(2997343227675854769)
XLA Ops:
  0.6 0.7 %pad_add_fusion.plan_ref = s32[40,128]{1,0:T(8,128)S(1)} fusion(s32[32,64]{1,0:T(8,128)} %bitcast.11, s32[8,128]{1,0:T(8,128)} %bitcast.6), kind=kLoop, calls=%fused_computation | loop fusion | flops 5120 | bytes 32768 | tf_op jit(solution)/shard_map/concatenate | solution.py:359
  1.4 0.0 copy-start.8
  1.4 0.0 copy-start
  1.4 0.0 copy-start.2
  1.4 0.0 copy-start.3
  1.4 1.9 %send_pack.1 = (f32[88,128]{1,0:T(8,128)S(1)}, f32[88,128]{1,0:T(8,128)S(1)}, f32[88,128]{1,0:T(8,128)S(1)}, f32[88,128]{1,0:T(8,128)S(1)}, f32[88,128]{1,0:T(8,...) custom-call(f32[162,1024]{1,0:T(8,128)} %x_hbm.1, s32[40,128]{1,0:T(8,128)S(1)} %pad_add_fusion.plan_ref), custom_call_target="tpu_custom_call" | custom-call | tf_op jit(solution)/shard_map/send_pack/pallas_call | solution.py:360
  3.3 0.0 copy-start.1
  3.3 2.5 %collective-permute-start = (f32[88,128]{1,0:T(8,128)S(1)}, f32[88,128]{1,0:T(8,128)S(1)}, u32[]{:S(2)}, u32[]{:S(2)}) collective-permute-start(f32[88,128]{1,0:T(8,128)S(1)} %get-tuple-element.19), channel_id=1, source_target_pairs={{0,8},{8,16},{16,24},{24,32},{32,40},{40,48},{48,56},{56,64},{64,7... | collective-permute-start | bytes 135176 | tf_op jit(solution)/shard_map/ppermute | solution.py:375
  5.9 6.5 %collective-permute-start.1 = (f32[88,128]{1,0:T(8,128)S(1)}, f32[88,128]{1,0:T(8,128)S(1)}, u32[]{:S(2)}, u32[]{:S(2)}) collective-permute-start(f32[88,128]{1,0:T(8,128)S(1)} %get-tuple-element.20), channel_id=1, source_target_pairs={{0,248},{8,0},{16,8},{24,16},{32,24},{40,32},{48,40},{56,48},{64,5... | collective-permute-start | bytes 135176 | tf_op jit(solution)/shard_map/ppermute | solution.py:375
  12.4 0.0 collective-permute-start.2
  12.4 5.7 %collective-permute-start.3 = (f32[88,128]{1,0:T(8,128)S(1)}, f32[88,128]{1,0:T(8,128)S(1)}, u32[]{:S(2)}, u32[]{:S(2)}) collective-permute-start(f32[88,128]{1,0:T(8,128)S(1)} %get-tuple-element.22), channel_id=1, source_target_pairs={{0,240},{8,248},{16,0},{24,8},{32,16},{40,24},{48,32},{56,40},{64,... | collective-permute-start | bytes 135176 | tf_op jit(solution)/shard_map/ppermute | solution.py:375
  18.1 0.0 collective-permute-start.4
  18.1 0.0 copy-done.8
  18.1 0.0 copy-start.6
  18.1 0.1 copy.13.cg_ref
  18.2 0.0 copy-done
  18.2 0.0 copy-done.2
  18.2 0.0 copy-done.3
  18.2 0.0 copy-done.1
  18.2 0.6 %copy-done.6 = f32[1024]{0:T(1024)S(1)} copy-done((f32[1024]{0:T(1024)S(1)}, f32[1024]{0:T(1024)}, u32[]{:S(2)}) %copy-start.6) | copy-done | bytes 4120
  18.8 0.0 copy-done.7
  18.8 0.1 copy-done.5
  18.9 0.0 copy-done.4
  18.9 7.3 %local_slots.1 = (f32[168,1024]{1,0:T(8,128)S(1)}, f32[168,1024]{1,0:T(8,128)S(1)}, f32[168,1024]{1,0:T(8,128)S(1)}, f32[168,128]{1,0:T(8,128)S(1)}, f32[2,8,1024]{2,1,0:T(8,128)S(1)}, /*index=5*/s32[8,1024]{1,0:T(8,128)S(1)}) custom-call(f32[168,1024]{1,0:T(8,128)S(1)} %get-tuple-element.24.x_ref, s32[88,1024]{1,0:T(8,128)S(1)} %get-tuple-element.25.packed, ...), custom_call_target="tpu_custom_call" | custom-call | flops 20000000 | bytes 4000000 | tf_op jit(solution)/shard_map/local_slots/pallas_call | solution.py:378
  26.1 0.0 collective-permute-done.g0
  26.1 0.0 collective-permute-done.1.g1
  26.1 0.0 collective-permute-done.2.g2
  26.2 0.0 collective-permute-done.3.g3
  26.2 0.0 collective-permute-done.4.g4
  26.2 2.9 %ghost_slots.1 = (f32[168,1024]{1,0:T(8,128)S(1)}, f32[8,16,128]{2,1,0:T(8,128)S(1)}) custom-call(f32[88,128]{1,0:T(8,128)S(1)} %collective-permute-done.g0, f32[88,128]{1,0:T(8,128)S(1)} %collective-permute-done.1.g1, f32[88,128]{1,0:T(8,128)S(1)} %collective-permute-done.2.g2, f32[88,128]{1,0:T(8,128)S(1)} %collective-permute-done.3.g3, ...), custom_call_target="tpu_custom_call" | custom-call | tf_op jit(solution)/shard_map/ghost_slots/pallas_call | solution.py:411
  29.1 10.5 %all_to_all.5.sums_ref = f32[8,16,128]{2,1,0:T(8,128)S(1)} all-to-all(f32[8,16,128]{2,1,0:T(8,128)S(1)} %get-tuple-element.31), channel_id=1, replica_groups=mesh['space'=32,'spec'=8] {'spec'}, dimensions={0} | all-to-all | bytes 131072 | tf_op jit(solution)/shard_map/all_to_all | solution.py:420
  39.6 1.5 %source.1 = (f32[162,1024]{1,0:T(8,128)}, f32[1,128]{1,0:T(1,128)}) custom-call(f32[8,16,128]{2,1,0:T(8,128)S(1)} %all_to_all.5.sums_ref, f32[168,1024]{1,0:T(8,128)S(1)} %get-tuple-element.32.adv_ref, f32[168,1024]{1,0:T(8,128)S(1)} %get-tuple-element.33.wind_ref, f32[168,128]{1,0:T(8,128)S(1)} %get-tuple-element.28.fc_ref), custom_call_target="tpu_custom_call" | custom-call | tf_op jit(solution)/shard_map/source/pallas_call | solution.py:421
  (3 shorter events, 0.0 us)
Async XLA Ops:
  1.4 16.7 %copy-start.8 = (f32[36,32]{0,1:T(8,128)S(1)}, f32[36,32]{0,1:T(8,128)}, u32[]{:S(2)}) copy-start(f32[36,32]{0,1:T(8,128)} %param.14) | copy-start | bytes 13828
  1.4 16.8 %copy-start = (f32[184,128]{1,0:T(8,128)S(1)}, f32[184,128]{1,0:T(8,128)}, u32[]{:S(2)}) copy-start(f32[184,128]{1,0:T(8,128)} %constant.4.clone.tab_ref) | copy-start | bytes 282628
  1.4 16.8 %copy-start.2 = (f32[8,1024]{1,0:T(8,128)S(1)}, f32[8,1024]{1,0:T(8,128)}, u32[]{:S(2)}) copy-start(f32[8,1024]{1,0:T(8,128)} %ew_ref.1) | copy-start | bytes 98308
  1.4 16.8 %copy-start.3 = (f32[8,1024]{1,0:T(8,128)S(1)}, f32[8,1024]{1,0:T(8,128)}, u32[]{:S(2)}) copy-start(f32[8,1024]{1,0:T(8,128)} %ea_ref.1) | copy-start | bytes 98308
  3.3 14.9 %copy-start.1 = (s32[8,1024]{1,0:T(8,128)S(1)}, s32[8,1024]{1,0:T(8,128)}, u32[]{:S(2)}) copy-start(s32[8,1024]{1,0:T(8,128)} %nb_ref.1) | copy-start | bytes 98308
  3.3 22.8 %collective-permute-start = (f32[88,128]{1,0:T(8,128)S(1)}, f32[88,128]{1,0:T(8,128)S(1)}, u32[]{:S(2)}, u32[]{:S(2)}) collective-permute-start(f32[88,128]{1,0:T(8,128)S(1)} %get-tuple-element.19), channel_id=1, source_target_pairs={{0,8},{8,16},{16,24},{24,32},{32,40},{40,48},{48,56},{56,64},{64,7... | collective-permute-start | bytes 135176 | tf_op jit(solution)/shard_map/ppermute | solution.py:375
  5.9 20.2 %collective-permute-start.1 = (f32[88,128]{1,0:T(8,128)S(1)}, f32[88,128]{1,0:T(8,128)S(1)}, u32[]{:S(2)}, u32[]{:S(2)}) collective-permute-start(f32[88,128]{1,0:T(8,128)S(1)} %get-tuple-element.20), channel_id=1, source_target_pairs={{0,248},{8,0},{16,8},{24,16},{32,24},{40,32},{48,40},{56,48},{64,5... | collective-permute-start | bytes 135176 | tf_op jit(solution)/shard_map/ppermute | solution.py:375
  12.4 13.8 %collective-permute-start.2 = (f32[88,128]{1,0:T(8,128)S(1)}, f32[88,128]{1,0:T(8,128)S(1)}, u32[]{:S(2)}, u32[]{:S(2)}) collective-permute-start(f32[88,128]{1,0:T(8,128)S(1)} %get-tuple-element.21), channel_id=1, source_target_pairs={{0,16},{8,24},{16,32},{24,40},{32,48},{40,56},{48,64},{56,72},{64,... | collective-permute-start | bytes 135176 | tf_op jit(solution)/shard_map/ppermute | solution.py:375
  12.4 13.8 %collective-permute-start.3 = (f32[88,128]{1,0:T(8,128)S(1)}, f32[88,128]{1,0:T(8,128)S(1)}, u32[]{:S(2)}, u32[]{:S(2)}) collective-permute-start(f32[88,128]{1,0:T(8,128)S(1)} %get-tuple-element.22), channel_id=1, source_target_pairs={{0,240},{8,248},{16,0},{24,8},{32,16},{40,24},{48,32},{56,40},{64,... | collective-permute-start | bytes 135176 | tf_op jit(solution)/shard_map/ppermute | solution.py:375
  18.1 8.1 %collective-permute-start.4 = (f32[88,128]{1,0:T(8,128)S(1)}, f32[88,128]{1,0:T(8,128)S(1)}, u32[]{:S(2)}, u32[]{:S(2)}) collective-permute-start(f32[88,128]{1,0:T(8,128)S(1)} %get-tuple-element.23), channel_id=1, source_target_pairs={{0,128},{8,136},{16,144},{24,152},{32,160},{40,168},{48,176},{56,1... | collective-permute-start | bytes 135176 | tf_op jit(solution)/shard_map/ppermute | solution.py:375
  18.1 0.7 %copy-start.6 = (f32[1024]{0:T(1024)S(1)}, f32[1024]{0:T(1024)}, u32[]{:S(2)}) copy-start(f32[1024]{0:T(1024)} %param.19) | copy-start | bytes 12292
  18.1 0.7 %copy-start.7 = (f32[1024]{0:T(1024)S(1)}, f32[1024]{0:T(1024)}, u32[]{:S(2)}) copy-start(f32[1024]{0:T(1024)} %param.20) | copy-start | bytes 12292
  18.2 0.7 %copy-start.5 = (s32[1024]{0:T(1024)S(1)}, s32[1024]{0:T(1024)}, u32[]{:S(2)}) copy-start(s32[1024]{0:T(1024)} %param.13) | copy-start | bytes 12292
  18.2 0.7 %copy-start.4 = (s32[1024]{0:T(1024)S(1)}, s32[1024]{0:T(1024)}, u32[]{:S(2)}) copy-start(s32[1024]{0:T(1024)} %param.12) | copy-start | bytes 12292

commit v3 on v2

--- a/solution.py
+++ b/solution.py
@@ -66,6 +66,10 @@
     return 1.0 - 2.0 * s * s, 2.0 * s * c
 
 
+MATRIX_SLOTS = 4
+GHOST_SLOTS = 3
+HALF = 176
+GHOST_HALF = 192
 CHUNKS = ((0, 6), (6, 11))
 
 
@@ -136,10 +140,10 @@
                 outs[4][rows, :] = jnp.where(low, top, bottom)
 
 
-def slots(packed, blocks, code, geo, tab_ref, lanes, bit_count):
+def slots(packed, blocks, code, geo, tab_ref, lanes, bit_count, product, columns, ready):
     total = [None] * 21
     shares = [None] * 9
-    for m in range(8):
+    for m in list(range(ready, 8)) + list(range(ready)):
         full = row8(code[m : m + 1, lanes])
         index = full & 127
         bits = [(full & (128 << i)) != 0 for i in range(bit_count)]
@@ -152,6 +156,15 @@
             for r in range(9)
         ]
         shares = [s if t is None else t + s for t, s in zip(shares, share)]
+        if m < ready:
+            for h in range(21):
+                half = product.shape[1] // 2
+                row = 8 * h + (8 if half > HALF and h > 10 else 0)
+                high = product[m, row : row + 8, columns]
+                low = product[m, half + row : half + row + 8, columns]
+                term = share[h % 9] * (high + low)
+                total[h] = term if total[h] is None else total[h] + term
+            continue
         for g in range(11):
             word = pick(
                 [packed[8 * g : 8 * g + 8, LANES * s : LANES * s + LANES] for s in range(blocks)],
@@ -163,6 +176,24 @@
                     term = share[h % 9] * value.astype(jnp.float32)
                     total[h] = term if total[h] is None else total[h] + term
     return total, shares
+
+
+def split(value):
+    high = value.astype(jnp.bfloat16)
+    return high, (value - high.astype(jnp.float32)).astype(jnp.bfloat16)
+
+
+def matrix_slots(count, code, pair, blocks, count_ref, hot_ref, parts_ref, product_ref):
+    size = count_ref.shape[0]
+    for m in range(count):
+        entry = code[m : m + 1, pair]
+        for j in range(blocks):
+            wanted = (entry - size * j).astype(jnp.float32).astype(jnp.bfloat16)
+            hit = count_ref[...] == jnp.broadcast_to(wanted, (size, 256))
+            hot_ref[m, size * j : size * j + size, :] = jnp.where(
+                hit, jnp.bfloat16(1), jnp.bfloat16(0)
+            )
+        product_ref[m] = jnp.dot(parts_ref[...], hot_ref[m], preferred_element_type=jnp.float32)
 
 
 def local_kernel(
@@ -186,6 +217,10 @@
     cgx,
     wloc,
     drive_ref,
+    parts_ref,
+    count_ref,
+    hot_ref,
+    product_ref,
 ):
     me = lax.axis_index("space")
     spec = lax.axis_index("spec")
@@ -228,11 +263,35 @@
         cgx[8 * g : 8 * g + 8, :] = cv
         fc_ref[8 * g : 8 * g + 8, :] = fv
 
-    def node_block(b, carry):
+    for g in range(11):
+        rows = slice(16 * g, 16 * g + 16)
+        for b in range(8):
+            lanes = slice(LANES * b, LANES * b + LANES)
+            if g < 10:
+                value = x_ref[rows, lanes] * SCALE
+            else:
+                value = jnp.concatenate(
+                    [x_ref[160:168, lanes] * SCALE, jnp.zeros((8, LANES), jnp.float32)], axis=0
+                )
+            parts_ref[rows, lanes], parts_ref[HALF + 16 * g : HALF + 16 * g + 16, lanes] = split(
+                value
+            )
+    count_ref[...] = lax.broadcasted_iota(jnp.int32, (256, 256), 0).astype(jnp.bfloat16)
+
+    def node_pair(p, carry):
+        pair = pl.ds(pl.multiple_of(p * 256, 256), 256)
+        matrix_slots(MATRIX_SLOTS, nb_ref, pair, 4, count_ref, hot_ref, parts_ref, product_ref)
+        for k in range(2):
+            node_block(2 * p + k, slice(LANES * k, LANES * k + LANES))
+        return carry
+
+    def node_block(b, columns):
         lanes = pl.ds(pl.multiple_of(b * LANES, LANES), LANES)
         wet = row8(wet_ref[pl.ds(b, 1), :].astype(jnp.float32))
         cls = row8(dc_ref[pl.ds(b, 1), :])
-        total, shares = slots(packed, 8, nb_ref, wloc, tab_ref, lanes, 3)
+        total, shares = slots(
+            packed, 8, nb_ref, wloc, tab_ref, lanes, 3, product_ref, columns, MATRIX_SLOTS
+        )
         dcos = row8(drive_ref[0, pl.ds(b, 1), :])
         dsin = row8(drive_ref[1, pl.ds(b, 1), :])
         for g in range(21):
@@ -244,14 +303,13 @@
             r = 8 * (g % 9)
             drive = tab_ref[r : r + 8, :] * dcos + tab_ref[72 + r : 80 + r, :] * dsin
             wind_ref[rows, lanes] = 0.125 * jnp.maximum(fc_ref[rows, :] * drive - 1.0, 0.0)
-        return carry
-
-    lax.fori_loop(0, 8, node_block, 0, unroll=2)
+
+    lax.fori_loop(0, 4, node_pair, 0, unroll=2)
 
 
 def ghost_kernel(
     g0, g1, g2, g3, g4, x_ref, base_ref, gain_ref, fc_ref, geo_ref, code_ref, tab_ref, adv_ref,
-    sums_ref, packed
+    sums_ref, packed, parts_ref, count_ref, hot_ref, product_ref
 ):
     low = lax.broadcasted_iota(jnp.int32, (8, LANES), 1) < GHOST
     for g in range(11):
@@ -265,9 +323,32 @@
                 word = jnp.where(low, word, (pltpu.roll(c, 64, 1) << 16) | c)
             packed[rows, LANES * q : LANES * q + LANES] = word
 
-    def node_block(b, carry):
+    zero = jnp.zeros((8, 3 * LANES), jnp.float32)
+    for h in range(2):
+        for g in range(0, 11, 2):
+            word = packed[8 * g : min(8 * g + 16, PACK), :]
+            value = (word & 65535) if h else lax.shift_right_logical(word, 16)
+            value = value.astype(jnp.float32)
+            if g == 10:
+                value = jnp.concatenate([value, zero], axis=0)
+            first = 96 * h + 8 * g
+            parts_ref[first : first + 16, :], parts_ref[
+                GHOST_HALF + first : GHOST_HALF + first + 16, :
+            ] = split(value)
+    count_ref[...] = lax.broadcasted_iota(jnp.int32, (LANES, 256), 0).astype(jnp.bfloat16)
+
+    def node_pair(p, carry):
+        pair = pl.ds(pl.multiple_of(p * 256, 256), 256)
+        matrix_slots(GHOST_SLOTS, code_ref, pair, 3, count_ref, hot_ref, parts_ref, product_ref)
+        for k in range(2):
+            node_block(2 * p + k, slice(LANES * k, LANES * k + LANES))
+        return carry
+
+    def node_block(b, columns):
         lanes = pl.ds(pl.multiple_of(b * LANES, LANES), LANES)
-        total, shares = slots(packed, 3, code_ref, geo_ref, tab_ref, lanes, 2)
+        total, shares = slots(
+            packed, 3, code_ref, geo_ref, tab_ref, lanes, 2, product_ref, columns, GHOST_SLOTS
+        )
         energy = jnp.zeros((8, LANES), jnp.float32)
         moment = jnp.zeros((8, LANES), jnp.float32)
         for g in range(21):
@@ -284,9 +365,8 @@
         for r in range(8):
             sums_ref[r, pl.ds(b, 1), :] = erow
             sums_ref[r, pl.ds(b + 8, 1), :] = mrow
-        return carry
-
-    lax.fori_loop(0, 8, node_block, 0, unroll=4)
+
+    lax.fori_loop(0, 4, node_pair, 0, unroll=2)
 
 
 OUT_ROWS = ((0, 5), (5, 10), (10, 15), (15, 21))
@@ -391,6 +471,10 @@
             pltpu.VMEM((168, LANES), F32),
             pltpu.VMEM((2, 8, 1024), F32),
             pltpu.VMEM((2, 8, LANES), F32),
+            pltpu.VMEM((2 * HALF, 1024), jnp.bfloat16),
+            pltpu.VMEM((256, 256), jnp.bfloat16),
+            pltpu.VMEM((MATRIX_SLOTS, 1024, 256), jnp.bfloat16),
+            pltpu.VMEM((MATRIX_SLOTS, 2 * HALF, 256), F32),
         ],
         compiler_params=LIMIT,
         cost_estimate=cost(20_000_000, 4_000_000),
@@ -413,7 +497,13 @@
         out_shape=(shape(168, 1024), shape(8, 16, LANES)),
         in_specs=[VMEM] * 12,
         out_specs=(VMEM,) * 2,
-        scratch_shapes=[pltpu.VMEM((PACK, 3 * LANES), I32)],
+        scratch_shapes=[
+            pltpu.VMEM((PACK, 3 * LANES), I32),
+            pltpu.VMEM((2 * GHOST_HALF, 3 * LANES), jnp.bfloat16),
+            pltpu.VMEM((LANES, 256), jnp.bfloat16),
+            pltpu.VMEM((GHOST_SLOTS, 3 * LANES, 256), jnp.bfloat16),
+            pltpu.VMEM((GHOST_SLOTS, 2 * GHOST_HALF, 256), F32),
+        ],
         compiler_params=LIMIT,
         name="ghost_slots",
     )(*ghosts, masked, base, gain, freq, geo, code, table)

time: 41.3 us -> 38.3 us (0.927)
  Pallas kernels: 13.6 us -> 10.4 us
    pallas_call x1, Pallas kernels: 7.26 us -> 4.55 us  [per_device(): pl.pallas_call(local_kernel, out_shape=(shape(168, 1024), shape(168, 1024...]
    pallas_call x1, Pallas kernels: 2.93 us -> 2.48 us  [per_device(): pl.pallas_call(ghost_kernel, out_shape=(shape(168, 1024), shape(8, 16, LA...]
  transfers between devices with their start and end apart: 5 -> 5, of which waited for: 0 -> 0; matrix products, arithmetic and copies ran while one was open for 0% -> 0% of each run, Pallas kernels for 18% -> 12%
where the time goes in v3:
time: 38.3 us; the launch traced here: 38 us
  starting transfers between devices  14.7 us (38%)
  blocking collectives  10.6 us (28%)
  Pallas kernels  10.4 us (27%)
  local copies, waits for them, and re-layouts  0.78 us (2%)
  between operations  0.76 us (2%)
  other arithmetic  0.73 us (2%)
    ppermute x5, starting transfers between devices, per_device(): lax.ppermute(outgoing[k], 'space', [(i, (i + o) % 32) for i in range(32)])  14.7 us
    all_to_all x1, blocking collectives, per_device(): lax.all_to_all(sums, 'spec', split_axis=0, concat_axis=0, tiled=True)  10.6 us
    pallas_call x1, Pallas kernels, per_device(): pl.pallas_call(local_kernel, out_shape=(shape(168, 1024), shape(168, 1024...  4.55 us
    pallas_call x1, Pallas kernels, per_device(): pl.pallas_call(ghost_kernel, out_shape=(shape(168, 1024), shape(8, 16, LA...  2.48 us
    pallas_call x1, Pallas kernels, per_device(): pl.pallas_call(send_kernel, out_shape=(shape(PACK, LANES),) * 5 + (shape(...  1.94 us
    pallas_call x1, Pallas kernels, per_device(): pl.pallas_call(source_kernel, out_shape=(shape(162, 1024), shape(1, LANES...  1.45 us
    unnamed x19, local copies, waits for them, and re-layouts  0.78 us
  transfers between devices with their start and end apart: 5, of which 0 were waited for; matrix products, arithmetic and copies ran while one was open for 0% of the time, Pallas kernels for 12%

profile of v3, /device:TPU:1, one launch (start us, length us, event | category | flops | bytes accessed | tf_op | source)
XLA Modules:
  0.0 38.0 jit_solution(8661538066045777764)
XLA Ops:
  0.6 0.7 %pad_add_fusion.plan_ref = s32[40,128]{1,0:T(8,128)S(1)} fusion(s32[32,64]{1,0:T(8,128)} %bitcast.11, s32[8,128]{1,0:T(8,128)} %bitcast.6), kind=kLoop, calls=%fused_computation | loop fusion | flops 5120 | bytes 32768 | tf_op jit(solution)/shard_map/concatenate | solution.py:439
  1.4 0.0 copy-start.8
  1.4 0.0 copy-start
  1.4 0.0 copy-start.2
  1.4 0.0 copy-start.3
  1.4 1.9 %send_pack.1 = (f32[88,128]{1,0:T(8,128)S(1)}, f32[88,128]{1,0:T(8,128)S(1)}, f32[88,128]{1,0:T(8,128)S(1)}, f32[88,128]{1,0:T(8,128)S(1)}, f32[88,128]{1,0:T(8,...) custom-call(f32[162,1024]{1,0:T(8,128)} %x_hbm.1, s32[40,128]{1,0:T(8,128)S(1)} %pad_add_fusion.plan_ref), custom_call_target="tpu_custom_call" | custom-call | tf_op jit(solution)/shard_map/send_pack/pallas_call | solution.py:440
  3.3 0.0 copy-start.1
  3.3 2.5 %collective-permute-start = (f32[88,128]{1,0:T(8,128)S(1)}, f32[88,128]{1,0:T(8,128)S(1)}, u32[]{:S(2)}, u32[]{:S(2)}) collective-permute-start(f32[88,128]{1,0:T(8,128)S(1)} %get-tuple-element.19), channel_id=1, source_target_pairs={{0,8},{8,16},{16,24},{24,32},{32,40},{40,48},{48,56},{56,64},{64,7... | collective-permute-start | bytes 135176 | tf_op jit(solution)/shard_map/ppermute | solution.py:455
  5.9 6.5 %collective-permute-start.1 = (f32[88,128]{1,0:T(8,128)S(1)}, f32[88,128]{1,0:T(8,128)S(1)}, u32[]{:S(2)}, u32[]{:S(2)}) collective-permute-start(f32[88,128]{1,0:T(8,128)S(1)} %get-tuple-element.20), channel_id=1, source_target_pairs={{0,248},{8,0},{16,8},{24,16},{32,24},{40,32},{48,40},{56,48},{64,5... | collective-permute-start | bytes 135176 | tf_op jit(solution)/shard_map/ppermute | solution.py:455
  12.4 0.0 collective-permute-start.2
  12.4 5.7 %collective-permute-start.3 = (f32[88,128]{1,0:T(8,128)S(1)}, f32[88,128]{1,0:T(8,128)S(1)}, u32[]{:S(2)}, u32[]{:S(2)}) collective-permute-start(f32[88,128]{1,0:T(8,128)S(1)} %get-tuple-element.22), channel_id=1, source_target_pairs={{0,240},{8,248},{16,0},{24,8},{32,16},{40,24},{48,32},{56,40},{64,... | collective-permute-start | bytes 135176 | tf_op jit(solution)/shard_map/ppermute | solution.py:455
  18.1 0.0 collective-permute-start.4
  18.1 0.0 copy-done.8
  18.1 0.0 copy-start.6
  18.1 0.1 copy.13.cg_ref
  18.2 0.0 copy-done
  18.2 0.0 copy-done.2
  18.2 0.0 copy-done.3
  18.2 0.0 copy-done.1
  18.2 0.6 %copy-done.6 = f32[1024]{0:T(1024)S(1)} copy-done((f32[1024]{0:T(1024)S(1)}, f32[1024]{0:T(1024)}, u32[]{:S(2)}) %copy-start.6) | copy-done | bytes 4120
  18.8 0.0 copy-done.7
  18.8 0.1 copy-done.5
  18.9 0.0 copy-done.4
  18.9 4.5 %local_slots.1 = (f32[168,1024]{1,0:T(8,128)S(1)}, f32[168,1024]{1,0:T(8,128)S(1)}, f32[168,1024]{1,0:T(8,128)S(1)}, f32[168,128]{1,0:T(8,128)S(1)}, f32[2,8,1024]{2,1,0:T(8,128)S(1)}, /*index=5*/s32[8,1024]{1,0:T(8,128)S(1)}) custom-call(f32[168,1024]{1,0:T(8,128)S(1)} %get-tuple-element.24.x_ref, s32[88,1024]{1,0:T(8,128)S(1)} %get-tuple-element.25.packed, ...), custom_call_target="tpu_custom_call" | custom-call | flops 20000000 | bytes 4000000 | tf_op jit(solution)/shard_map/local_slots/pallas_call | solution.py:458
  23.4 0.0 collective-permute-done.g0
  23.4 0.0 collective-permute-done.1.g1
  23.4 0.0 collective-permute-done.2.g2
  23.5 0.0 collective-permute-done.3.g3
  23.5 0.0 collective-permute-done.4.g4
  23.5 2.5 %ghost_slots.1 = (f32[168,1024]{1,0:T(8,128)S(1)}, f32[8,16,128]{2,1,0:T(8,128)S(1)}) custom-call(f32[88,128]{1,0:T(8,128)S(1)} %collective-permute-done.g0, f32[88,128]{1,0:T(8,128)S(1)} %collective-permute-done.1.g1, f32[88,128]{1,0:T(8,128)S(1)} %collective-permute-done.2.g2, f32[88,128]{1,0:T(8,128)S(1)} %collective-permute-done.3.g3, ...), custom_call_target="tpu_custom_call" | custom-call | tf_op jit(solution)/shard_map/ghost_slots/pallas_call | solution.py:495
  25.9 10.6 %all_to_all.5.sums_ref = f32[8,16,128]{2,1,0:T(8,128)S(1)} all-to-all(f32[8,16,128]{2,1,0:T(8,128)S(1)} %get-tuple-element.31), channel_id=1, replica_groups=mesh['space'=32,'spec'=8] {'spec'}, dimensions={0} | all-to-all | bytes 131072 | tf_op jit(solution)/shard_map/all_to_all | solution.py:510
  36.5 1.5 %source.1 = (f32[162,1024]{1,0:T(8,128)}, f32[1,128]{1,0:T(1,128)}) custom-call(f32[8,16,128]{2,1,0:T(8,128)S(1)} %all_to_all.5.sums_ref, f32[168,1024]{1,0:T(8,128)S(1)} %get-tuple-element.32.adv_ref, f32[168,1024]{1,0:T(8,128)S(1)} %get-tuple-element.33.wind_ref, f32[168,128]{1,0:T(8,128)S(1)} %get-tuple-element.28.fc_ref), custom_call_target="tpu_custom_call" | custom-call | tf_op jit(solution)/shard_map/source/pallas_call | solution.py:511
  (3 shorter events, 0.0 us)
Async XLA Ops:
  1.4 16.7 %copy-start.8 = (f32[36,32]{0,1:T(8,128)S(1)}, f32[36,32]{0,1:T(8,128)}, u32[]{:S(2)}) copy-start(f32[36,32]{0,1:T(8,128)} %param.14) | copy-start | bytes 13828
  1.4 16.8 %copy-start = (f32[184,128]{1,0:T(8,128)S(1)}, f32[184,128]{1,0:T(8,128)}, u32[]{:S(2)}) copy-start(f32[184,128]{1,0:T(8,128)} %constant.4.clone.tab_ref) | copy-start | bytes 282628
  1.4 16.8 %copy-start.2 = (f32[8,1024]{1,0:T(8,128)S(1)}, f32[8,1024]{1,0:T(8,128)}, u32[]{:S(2)}) copy-start(f32[8,1024]{1,0:T(8,128)} %ew_ref.1) | copy-start | bytes 98308
  1.4 16.8 %copy-start.3 = (f32[8,1024]{1,0:T(8,128)S(1)}, f32[8,1024]{1,0:T(8,128)}, u32[]{:S(2)}) copy-start(f32[8,1024]{1,0:T(8,128)} %ea_ref.1) | copy-start | bytes 98308
  3.3 14.9 %copy-start.1 = (s32[8,1024]{1,0:T(8,128)S(1)}, s32[8,1024]{1,0:T(8,128)}, u32[]{:S(2)}) copy-start(s32[8,1024]{1,0:T(8,128)} %nb_ref.1) | copy-start | bytes 98308
  3.3 20.1 %collective-permute-start = (f32[88,128]{1,0:T(8,128)S(1)}, f32[88,128]{1,0:T(8,128)S(1)}, u32[]{:S(2)}, u32[]{:S(2)}) collective-permute-start(f32[88,128]{1,0:T(8,128)S(1)} %get-tuple-element.19), channel_id=1, source_target_pairs={{0,8},{8,16},{16,24},{24,32},{32,40},{40,48},{48,56},{56,64},{64,7... | collective-permute-start | bytes 135176 | tf_op jit(solution)/shard_map/ppermute | solution.py:455
  5.9 17.5 %collective-permute-start.1 = (f32[88,128]{1,0:T(8,128)S(1)}, f32[88,128]{1,0:T(8,128)S(1)}, u32[]{:S(2)}, u32[]{:S(2)}) collective-permute-start(f32[88,128]{1,0:T(8,128)S(1)} %get-tuple-element.20), channel_id=1, source_target_pairs={{0,248},{8,0},{16,8},{24,16},{32,24},{40,32},{48,40},{56,48},{64,5... | collective-permute-start | bytes 135176 | tf_op jit(solution)/shard_map/ppermute | solution.py:455
  12.4 11.1 %collective-permute-start.2 = (f32[88,128]{1,0:T(8,128)S(1)}, f32[88,128]{1,0:T(8,128)S(1)}, u32[]{:S(2)}, u32[]{:S(2)}) collective-permute-start(f32[88,128]{1,0:T(8,128)S(1)} %get-tuple-element.21), channel_id=1, source_target_pairs={{0,16},{8,24},{16,32},{24,40},{32,48},{40,56},{48,64},{56,72},{64,... | collective-permute-start | bytes 135176 | tf_op jit(solution)/shard_map/ppermute | solution.py:455
  12.4 11.1 %collective-permute-start.3 = (f32[88,128]{1,0:T(8,128)S(1)}, f32[88,128]{1,0:T(8,128)S(1)}, u32[]{:S(2)}, u32[]{:S(2)}) collective-permute-start(f32[88,128]{1,0:T(8,128)S(1)} %get-tuple-element.22), channel_id=1, source_target_pairs={{0,240},{8,248},{16,0},{24,8},{32,16},{40,24},{48,32},{56,40},{64,... | collective-permute-start | bytes 135176 | tf_op jit(solution)/shard_map/ppermute | solution.py:455
  18.1 5.4 %collective-permute-start.4 = (f32[88,128]{1,0:T(8,128)S(1)}, f32[88,128]{1,0:T(8,128)S(1)}, u32[]{:S(2)}, u32[]{:S(2)}) collective-permute-start(f32[88,128]{1,0:T(8,128)S(1)} %get-tuple-element.23), channel_id=1, source_target_pairs={{0,128},{8,136},{16,144},{24,152},{32,160},{40,168},{48,176},{56,1... | collective-permute-start | bytes 135176 | tf_op jit(solution)/shard_map/ppermute | solution.py:455
  18.1 0.7 %copy-start.6 = (f32[1024]{0:T(1024)S(1)}, f32[1024]{0:T(1024)}, u32[]{:S(2)}) copy-start(f32[1024]{0:T(1024)} %param.19) | copy-start | bytes 12292
  18.1 0.7 %copy-start.7 = (f32[1024]{0:T(1024)S(1)}, f32[1024]{0:T(1024)}, u32[]{:S(2)}) copy-start(f32[1024]{0:T(1024)} %param.20) | copy-start | bytes 12292
  18.2 0.7 %copy-start.5 = (s32[1024]{0:T(1024)S(1)}, s32[1024]{0:T(1024)}, u32[]{:S(2)}) copy-start(s32[1024]{0:T(1024)} %param.13) | copy-start | bytes 12292
  18.2 0.7 %copy-start.4 = (s32[1024]{0:T(1024)S(1)}, s32[1024]{0:T(1024)}, u32[]{:S(2)}) copy-start(s32[1024]{0:T(1024)} %param.12) | copy-start | bytes 12292

commit v4 on v3

--- a/solution.py
+++ b/solution.py
@@ -337,36 +337,49 @@
             ] = split(value)
     count_ref[...] = lax.broadcasted_iota(jnp.int32, (LANES, 256), 0).astype(jnp.bfloat16)
 
-    def node_pair(p, carry):
-        pair = pl.ds(pl.multiple_of(p * 256, 256), 256)
-        matrix_slots(GHOST_SLOTS, code_ref, pair, 3, count_ref, hot_ref, parts_ref, product_ref)
+    for p in range(4):
+        matrix_slots(
+            GHOST_SLOTS,
+            code_ref,
+            slice(256 * p, 256 * p + 256),
+            3,
+            count_ref,
+            hot_ref.at[p % 2],
+            parts_ref,
+            product_ref.at[p % 2],
+        )
         for k in range(2):
-            node_block(2 * p + k, slice(LANES * k, LANES * k + LANES))
-        return carry
-
-    def node_block(b, columns):
-        lanes = pl.ds(pl.multiple_of(b * LANES, LANES), LANES)
-        total, shares = slots(
-            packed, 3, code_ref, geo_ref, tab_ref, lanes, 2, product_ref, columns, GHOST_SLOTS
-        )
-        energy = jnp.zeros((8, LANES), jnp.float32)
-        moment = jnp.zeros((8, LANES), jnp.float32)
-        for g in range(21):
-            rows = slice(8 * g, 8 * g + 8)
-            inflow = total[g] * (1.0 / SCALE) - x_ref[rows, lanes] * shares[g % 9]
-            adv = base_ref[rows, lanes] + gain_ref[rows, lanes] * inflow
-            adv_ref[rows, lanes] = adv
-            freq = fc_ref[rows, :]
-            term = freq * adv
-            energy = energy + term
-            moment = moment + freq * term
-        erow = jnp.sum(energy, axis=0, keepdims=True) * _KAPPA
-        mrow = jnp.sum(moment, axis=0, keepdims=True) * _KAPPA
-        for r in range(8):
-            sums_ref[r, pl.ds(b, 1), :] = erow
-            sums_ref[r, pl.ds(b + 8, 1), :] = mrow
-
-    lax.fori_loop(0, 4, node_pair, 0, unroll=2)
+            b = 2 * p + k
+            columns = slice(LANES * k, LANES * k + LANES)
+            lanes = slice(LANES * b, LANES * b + LANES)
+            total, shares = slots(
+                packed,
+                3,
+                code_ref,
+                geo_ref,
+                tab_ref,
+                lanes,
+                2,
+                product_ref.at[p % 2],
+                columns,
+                GHOST_SLOTS,
+            )
+            energy = jnp.zeros((8, LANES), jnp.float32)
+            moment = jnp.zeros((8, LANES), jnp.float32)
+            for g in range(21):
+                rows = slice(8 * g, 8 * g + 8)
+                inflow = total[g] * (1.0 / SCALE) - x_ref[rows, lanes] * shares[g % 9]
+                adv = base_ref[rows, lanes] + gain_ref[rows, lanes] * inflow
+                adv_ref[rows, lanes] = adv
+                freq = fc_ref[rows, :]
+                term = freq * adv
+                energy = energy + term
+                moment = moment + freq * term
+            erow = jnp.sum(energy, axis=0, keepdims=True) * _KAPPA
+            mrow = jnp.sum(moment, axis=0, keepdims=True) * _KAPPA
+            for r in range(8):
+                sums_ref[r, b : b + 1, :] = erow
+                sums_ref[r, b + 8 : b + 9, :] = mrow
 
 
 OUT_ROWS = ((0, 5), (5, 10), (10, 15), (15, 21))
@@ -501,8 +514,8 @@
             pltpu.VMEM((PACK, 3 * LANES), I32),
             pltpu.VMEM((2 * GHOST_HALF, 3 * LANES), jnp.bfloat16),
             pltpu.VMEM((LANES, 256), jnp.bfloat16),
-            pltpu.VMEM((GHOST_SLOTS, 3 * LANES, 256), jnp.bfloat16),
-            pltpu.VMEM((GHOST_SLOTS, 2 * GHOST_HALF, 256), F32),
+            pltpu.VMEM((2, GHOST_SLOTS, 3 * LANES, 256), jnp.bfloat16),
+            pltpu.VMEM((2, GHOST_SLOTS, 2 * GHOST_HALF, 256), F32),
         ],
         compiler_params=LIMIT,
         name="ghost_slots",

time: 38.3 us -> 38.1 us (level)
  no operation moved by 1% of the time
where the time goes in v4:
time: 38.1 us; the launch traced here: 37.8 us
  starting transfers between devices  14.7 us (39%)
  blocking collectives  10.6 us (28%)
  Pallas kernels  10.2 us (27%)
  local copies, waits for them, and re-layouts  0.78 us (2%)
  between operations  0.75 us (2%)
  other arithmetic  0.73 us (2%)
    ppermute x5, starting transfers between devices, per_device(): lax.ppermute(outgoing[k], 'space', [(i, (i + o) % 32) for i in range(32)])  14.7 us
    all_to_all x1, blocking collectives, per_device(): lax.all_to_all(sums, 'spec', split_axis=0, concat_axis=0, tiled=True)  10.6 us
    pallas_call x1, Pallas kernels, per_device(): pl.pallas_call(local_kernel, out_shape=(shape(168, 1024), shape(168, 1024...  4.55 us
    pallas_call x1, Pallas kernels, per_device(): pl.pallas_call(ghost_kernel, out_shape=(shape(168, 1024), shape(8, 16, LA...  2.28 us
    pallas_call x1, Pallas kernels, per_device(): pl.pallas_call(send_kernel, out_shape=(shape(PACK, LANES),) * 5 + (shape(...  1.94 us
    pallas_call x1, Pallas kernels, per_device(): pl.pallas_call(source_kernel, out_shape=(shape(162, 1024), shape(1, LANES...  1.45 us
    unnamed x19, local copies, waits for them, and re-layouts  0.78 us
  transfers between devices with their start and end apart: 5, of which 0 were waited for; matrix products, arithmetic and copies ran while one was open for 0% of the time, Pallas kernels for 12%

profile of v4, /device:TPU:1, one launch (start us, length us, event | category | flops | bytes accessed | tf_op | source)
XLA Modules:
  0.0 37.8 jit_solution(8931804247133932356)
XLA Ops:
  0.6 0.7 %pad_add_fusion.plan_ref = s32[40,128]{1,0:T(8,128)S(1)} fusion(s32[32,64]{1,0:T(8,128)} %bitcast.11, s32[8,128]{1,0:T(8,128)} %bitcast.6), kind=kLoop, calls=%fused_computation | loop fusion | flops 5120 | bytes 32768 | tf_op jit(solution)/shard_map/concatenate | solution.py:452
  1.4 0.0 copy-start.8
  1.4 0.0 copy-start
  1.4 0.0 copy-start.2
  1.4 0.0 copy-start.3
  1.4 1.9 %send_pack.1 = (f32[88,128]{1,0:T(8,128)S(1)}, f32[88,128]{1,0:T(8,128)S(1)}, f32[88,128]{1,0:T(8,128)S(1)}, f32[88,128]{1,0:T(8,128)S(1)}, f32[88,128]{1,0:T(8,...) custom-call(f32[162,1024]{1,0:T(8,128)} %x_hbm.1, s32[40,128]{1,0:T(8,128)S(1)} %pad_add_fusion.plan_ref), custom_call_target="tpu_custom_call" | custom-call | tf_op jit(solution)/shard_map/send_pack/pallas_call | solution.py:453
  3.3 0.0 copy-start.1
  3.3 2.5 %collective-permute-start = (f32[88,128]{1,0:T(8,128)S(1)}, f32[88,128]{1,0:T(8,128)S(1)}, u32[]{:S(2)}, u32[]{:S(2)}) collective-permute-start(f32[88,128]{1,0:T(8,128)S(1)} %get-tuple-element.19), channel_id=1, source_target_pairs={{0,8},{8,16},{16,24},{24,32},{32,40},{40,48},{48,56},{56,64},{64,7... | collective-permute-start | bytes 135176 | tf_op jit(solution)/shard_map/ppermute | solution.py:468
  5.9 6.5 %collective-permute-start.1 = (f32[88,128]{1,0:T(8,128)S(1)}, f32[88,128]{1,0:T(8,128)S(1)}, u32[]{:S(2)}, u32[]{:S(2)}) collective-permute-start(f32[88,128]{1,0:T(8,128)S(1)} %get-tuple-element.20), channel_id=1, source_target_pairs={{0,248},{8,0},{16,8},{24,16},{32,24},{40,32},{48,40},{56,48},{64,5... | collective-permute-start | bytes 135176 | tf_op jit(solution)/shard_map/ppermute | solution.py:468
  12.4 0.0 collective-permute-start.2
  12.4 5.7 %collective-permute-start.3 = (f32[88,128]{1,0:T(8,128)S(1)}, f32[88,128]{1,0:T(8,128)S(1)}, u32[]{:S(2)}, u32[]{:S(2)}) collective-permute-start(f32[88,128]{1,0:T(8,128)S(1)} %get-tuple-element.22), channel_id=1, source_target_pairs={{0,240},{8,248},{16,0},{24,8},{32,16},{40,24},{48,32},{56,40},{64,... | collective-permute-start | bytes 135176 | tf_op jit(solution)/shard_map/ppermute | solution.py:468
  18.1 0.0 collective-permute-start.4
  18.1 0.0 copy-done.8
  18.1 0.0 copy-start.6
  18.1 0.1 copy.13.cg_ref
  18.2 0.0 copy-done
  18.2 0.0 copy-done.2
  18.2 0.0 copy-done.3
  18.2 0.0 copy-done.1
  18.2 0.6 %copy-done.6 = f32[1024]{0:T(1024)S(1)} copy-done((f32[1024]{0:T(1024)S(1)}, f32[1024]{0:T(1024)}, u32[]{:S(2)}) %copy-start.6) | copy-done | bytes 4120
  18.8 0.0 copy-done.7
  18.8 0.1 copy-done.5
  18.9 0.0 copy-done.4
  18.9 4.5 %local_slots.1 = (f32[168,1024]{1,0:T(8,128)S(1)}, f32[168,1024]{1,0:T(8,128)S(1)}, f32[168,1024]{1,0:T(8,128)S(1)}, f32[168,128]{1,0:T(8,128)S(1)}, f32[2,8,1024]{2,1,0:T(8,128)S(1)}, /*index=5*/s32[8,1024]{1,0:T(8,128)S(1)}) custom-call(f32[168,1024]{1,0:T(8,128)S(1)} %get-tuple-element.24.x_ref, s32[88,1024]{1,0:T(8,128)S(1)} %get-tuple-element.25.packed, ...), custom_call_target="tpu_custom_call" | custom-call | flops 20000000 | bytes 4000000 | tf_op jit(solution)/shard_map/local_slots/pallas_call | solution.py:471
  23.4 0.0 collective-permute-done.g0
  23.4 0.0 collective-permute-done.1.g1
  23.4 0.0 collective-permute-done.2.g2
  23.5 0.0 collective-permute-done.3.g3
  23.5 0.0 collective-permute-done.4.g4
  23.5 2.3 %ghost_slots.1 = (f32[168,1024]{1,0:T(8,128)S(1)}, f32[8,16,128]{2,1,0:T(8,128)S(1)}) custom-call(f32[88,128]{1,0:T(8,128)S(1)} %collective-permute-done.g0, f32[88,128]{1,0:T(8,128)S(1)} %collective-permute-done.1.g1, f32[88,128]{1,0:T(8,128)S(1)} %collective-permute-done.2.g2, f32[88,128]{1,0:T(8,128)S(1)} %collective-permute-done.3.g3, ...), custom_call_target="tpu_custom_call" | custom-call | tf_op jit(solution)/shard_map/ghost_slots/pallas_call | solution.py:508
  25.7 10.6 %all_to_all.5.sums_ref = f32[8,16,128]{2,1,0:T(8,128)S(1)} all-to-all(f32[8,16,128]{2,1,0:T(8,128)S(1)} %get-tuple-element.31), channel_id=1, replica_groups=mesh['space'=32,'spec'=8] {'spec'}, dimensions={0} | all-to-all | bytes 131072 | tf_op jit(solution)/shard_map/all_to_all | solution.py:523
  36.3 1.5 %source.1 = (f32[162,1024]{1,0:T(8,128)}, f32[1,128]{1,0:T(1,128)}) custom-call(f32[8,16,128]{2,1,0:T(8,128)S(1)} %all_to_all.5.sums_ref, f32[168,1024]{1,0:T(8,128)S(1)} %get-tuple-element.32.adv_ref, f32[168,1024]{1,0:T(8,128)S(1)} %get-tuple-element.33.wind_ref, f32[168,128]{1,0:T(8,128)S(1)} %get-tuple-element.28.fc_ref), custom_call_target="tpu_custom_call" | custom-call | tf_op jit(solution)/shard_map/source/pallas_call | solution.py:524
  (3 shorter events, 0.0 us)
Async XLA Ops:
  1.4 16.7 %copy-start.8 = (f32[36,32]{0,1:T(8,128)S(1)}, f32[36,32]{0,1:T(8,128)}, u32[]{:S(2)}) copy-start(f32[36,32]{0,1:T(8,128)} %param.14) | copy-start | bytes 13828
  1.4 16.8 %copy-start = (f32[184,128]{1,0:T(8,128)S(1)}, f32[184,128]{1,0:T(8,128)}, u32[]{:S(2)}) copy-start(f32[184,128]{1,0:T(8,128)} %constant.4.clone.tab_ref) | copy-start | bytes 282628
  1.4 16.8 %copy-start.2 = (f32[8,1024]{1,0:T(8,128)S(1)}, f32[8,1024]{1,0:T(8,128)}, u32[]{:S(2)}) copy-start(f32[8,1024]{1,0:T(8,128)} %ew_ref.1) | copy-start | bytes 98308
  1.4 16.8 %copy-start.3 = (f32[8,1024]{1,0:T(8,128)S(1)}, f32[8,1024]{1,0:T(8,128)}, u32[]{:S(2)}) copy-start(f32[8,1024]{1,0:T(8,128)} %ea_ref.1) | copy-start | bytes 98308
  3.3 14.9 %copy-start.1 = (s32[8,1024]{1,0:T(8,128)S(1)}, s32[8,1024]{1,0:T(8,128)}, u32[]{:S(2)}) copy-start(s32[8,1024]{1,0:T(8,128)} %nb_ref.1) | copy-start | bytes 98308
  3.3 20.1 %collective-permute-start = (f32[88,128]{1,0:T(8,128)S(1)}, f32[88,128]{1,0:T(8,128)S(1)}, u32[]{:S(2)}, u32[]{:S(2)}) collective-permute-start(f32[88,128]{1,0:T(8,128)S(1)} %get-tuple-element.19), channel_id=1, source_target_pairs={{0,8},{8,16},{16,24},{24,32},{32,40},{40,48},{48,56},{56,64},{64,7... | collective-permute-start | bytes 135176 | tf_op jit(solution)/shard_map/ppermute | solution.py:468
  5.9 17.5 %collective-permute-start.1 = (f32[88,128]{1,0:T(8,128)S(1)}, f32[88,128]{1,0:T(8,128)S(1)}, u32[]{:S(2)}, u32[]{:S(2)}) collective-permute-start(f32[88,128]{1,0:T(8,128)S(1)} %get-tuple-element.20), channel_id=1, source_target_pairs={{0,248},{8,0},{16,8},{24,16},{32,24},{40,32},{48,40},{56,48},{64,5... | collective-permute-start | bytes 135176 | tf_op jit(solution)/shard_map/ppermute | solution.py:468
  12.4 11.1 %collective-permute-start.2 = (f32[88,128]{1,0:T(8,128)S(1)}, f32[88,128]{1,0:T(8,128)S(1)}, u32[]{:S(2)}, u32[]{:S(2)}) collective-permute-start(f32[88,128]{1,0:T(8,128)S(1)} %get-tuple-element.21), channel_id=1, source_target_pairs={{0,16},{8,24},{16,32},{24,40},{32,48},{40,56},{48,64},{56,72},{64,... | collective-permute-start | bytes 135176 | tf_op jit(solution)/shard_map/ppermute | solution.py:468
  12.4 11.1 %collective-permute-start.3 = (f32[88,128]{1,0:T(8,128)S(1)}, f32[88,128]{1,0:T(8,128)S(1)}, u32[]{:S(2)}, u32[]{:S(2)}) collective-permute-start(f32[88,128]{1,0:T(8,128)S(1)} %get-tuple-element.22), channel_id=1, source_target_pairs={{0,240},{8,248},{16,0},{24,8},{32,16},{40,24},{48,32},{56,40},{64,... | collective-permute-start | bytes 135176 | tf_op jit(solution)/shard_map/ppermute | solution.py:468
  18.1 5.4 %collective-permute-start.4 = (f32[88,128]{1,0:T(8,128)S(1)}, f32[88,128]{1,0:T(8,128)S(1)}, u32[]{:S(2)}, u32[]{:S(2)}) collective-permute-start(f32[88,128]{1,0:T(8,128)S(1)} %get-tuple-element.23), channel_id=1, source_target_pairs={{0,128},{8,136},{16,144},{24,152},{32,160},{40,168},{48,176},{56,1... | collective-permute-start | bytes 135176 | tf_op jit(solution)/shard_map/ppermute | solution.py:468
  18.1 0.7 %copy-start.6 = (f32[1024]{0:T(1024)S(1)}, f32[1024]{0:T(1024)}, u32[]{:S(2)}) copy-start(f32[1024]{0:T(1024)} %param.19) | copy-start | bytes 12292
  18.1 0.7 %copy-start.7 = (f32[1024]{0:T(1024)S(1)}, f32[1024]{0:T(1024)}, u32[]{:S(2)}) copy-start(f32[1024]{0:T(1024)} %param.20) | copy-start | bytes 12292
  18.2 0.7 %copy-start.5 = (s32[1024]{0:T(1024)S(1)}, s32[1024]{0:T(1024)}, u32[]{:S(2)}) copy-start(s32[1024]{0:T(1024)} %param.13) | copy-start | bytes 12292
  18.2 0.7 %copy-start.4 = (s32[1024]{0:T(1024)S(1)}, s32[1024]{0:T(1024)}, u32[]{:S(2)}) copy-start(s32[1024]{0:T(1024)} %param.12) | copy-start | bytes 12292

commit v5 on v4

--- a/solution.py
+++ b/solution.py
@@ -278,19 +278,12 @@
             )
     count_ref[...] = lax.broadcasted_iota(jnp.int32, (256, 256), 0).astype(jnp.bfloat16)
 
-    def node_pair(p, carry):
-        pair = pl.ds(pl.multiple_of(p * 256, 256), 256)
-        matrix_slots(MATRIX_SLOTS, nb_ref, pair, 4, count_ref, hot_ref, parts_ref, product_ref)
-        for k in range(2):
-            node_block(2 * p + k, slice(LANES * k, LANES * k + LANES))
-        return carry
-
-    def node_block(b, columns):
-        lanes = pl.ds(pl.multiple_of(b * LANES, LANES), LANES)
+    def node_block(b, columns, product):
+        lanes = slice(LANES * b, LANES * b + LANES)
         wet = row8(wet_ref[pl.ds(b, 1), :].astype(jnp.float32))
         cls = row8(dc_ref[pl.ds(b, 1), :])
         total, shares = slots(
-            packed, 8, nb_ref, wloc, tab_ref, lanes, 3, product_ref, columns, MATRIX_SLOTS
+            packed, 8, nb_ref, wloc, tab_ref, lanes, 3, product, columns, MATRIX_SLOTS
         )
         dcos = row8(drive_ref[0, pl.ds(b, 1), :])
         dsin = row8(drive_ref[1, pl.ds(b, 1), :])
@@ -304,7 +297,12 @@
             drive = tab_ref[r : r + 8, :] * dcos + tab_ref[72 + r : 80 + r, :] * dsin
             wind_ref[rows, lanes] = 0.125 * jnp.maximum(fc_ref[rows, :] * drive - 1.0, 0.0)
 
-    lax.fori_loop(0, 4, node_pair, 0, unroll=2)
+    for p in range(4):
+        hot, product = hot_ref.at[p % 2], product_ref.at[p % 2]
+        pair = slice(256 * p, 256 * p + 256)
+        matrix_slots(MATRIX_SLOTS, nb_ref, pair, 4, count_ref, hot, parts_ref, product)
+        for k in range(2):
+            node_block(2 * p + k, slice(LANES * k, LANES * k + LANES), product)
 
 
 def ghost_kernel(
@@ -486,8 +484,8 @@
             pltpu.VMEM((2, 8, LANES), F32),
             pltpu.VMEM((2 * HALF, 1024), jnp.bfloat16),
             pltpu.VMEM((256, 256), jnp.bfloat16),
-            pltpu.VMEM((MATRIX_SLOTS, 1024, 256), jnp.bfloat16),
-            pltpu.VMEM((MATRIX_SLOTS, 2 * HALF, 256), F32),
+            pltpu.VMEM((2, MATRIX_SLOTS, 1024, 256), jnp.bfloat16),
+            pltpu.VMEM((2, MATRIX_SLOTS, 2 * HALF, 256), F32),
         ],
         compiler_params=LIMIT,
         cost_estimate=cost(20_000_000, 4_000_000),

time: 38.1 us -> 38.1 us (level)
  no operation moved by 1% of the time
where the time goes in v5:
time: 38.1 us; the launch traced here: 37.8 us
  starting transfers between devices  14.7 us (39%)
  blocking collectives  10.6 us (28%)
  Pallas kernels  10.2 us (27%)
  local copies, waits for them, and re-layouts  0.78 us (2%)
  between operations  0.75 us (2%)
  other arithmetic  0.73 us (2%)
    ppermute x5, starting transfers between devices, per_device(): lax.ppermute(outgoing[k], 'space', [(i, (i + o) % 32) for i in range(32)])  14.7 us
    all_to_all x1, blocking collectives, per_device(): lax.all_to_all(sums, 'spec', split_axis=0, concat_axis=0, tiled=True)  10.6 us
    pallas_call x1, Pallas kernels, per_device(): pl.pallas_call(local_kernel, out_shape=(shape(168, 1024), shape(168, 1024...  4.5 us
    pallas_call x1, Pallas kernels, per_device(): pl.pallas_call(ghost_kernel, out_shape=(shape(168, 1024), shape(8, 16, LA...  2.28 us
    pallas_call x1, Pallas kernels, per_device(): pl.pallas_call(send_kernel, out_shape=(shape(PACK, LANES),) * 5 + (shape(...  1.94 us
    pallas_call x1, Pallas kernels, per_device(): pl.pallas_call(source_kernel, out_shape=(shape(162, 1024), shape(1, LANES...  1.45 us
    unnamed x19, local copies, waits for them, and re-layouts  0.78 us
  transfers between devices with their start and end apart: 5, of which 0 were waited for; matrix products, arithmetic and copies ran while one was open for 0% of the time, Pallas kernels for 12%

profile of v5, /device:TPU:1, one launch (start us, length us, event | category | flops | bytes accessed | tf_op | source)
XLA Modules:
  0.0 37.8 jit_solution(10665250064713466524)
XLA Ops:
  0.6 0.7 %pad_add_fusion.plan_ref = s32[40,128]{1,0:T(8,128)S(1)} fusion(s32[32,64]{1,0:T(8,128)} %bitcast.11, s32[8,128]{1,0:T(8,128)} %bitcast.6), kind=kLoop, calls=%fused_computation | loop fusion | flops 5120 | bytes 32768 | tf_op jit(solution)/shard_map/concatenate | solution.py:450
  1.4 0.0 copy-start.8
  1.4 0.0 copy-start
  1.4 0.0 copy-start.2
  1.4 0.0 copy-start.3
  1.4 1.9 %send_pack.1 = (f32[88,128]{1,0:T(8,128)S(1)}, f32[88,128]{1,0:T(8,128)S(1)}, f32[88,128]{1,0:T(8,128)S(1)}, f32[88,128]{1,0:T(8,128)S(1)}, f32[88,128]{1,0:T(8,...) custom-call(f32[162,1024]{1,0:T(8,128)} %x_hbm.1, s32[40,128]{1,0:T(8,128)S(1)} %pad_add_fusion.plan_ref), custom_call_target="tpu_custom_call" | custom-call | tf_op jit(solution)/shard_map/send_pack/pallas_call | solution.py:451
  3.3 0.0 copy-start.1
  3.3 2.5 %collective-permute-start = (f32[88,128]{1,0:T(8,128)S(1)}, f32[88,128]{1,0:T(8,128)S(1)}, u32[]{:S(2)}, u32[]{:S(2)}) collective-permute-start(f32[88,128]{1,0:T(8,128)S(1)} %get-tuple-element.19), channel_id=1, source_target_pairs={{0,8},{8,16},{16,24},{24,32},{32,40},{40,48},{48,56},{56,64},{64,7... | collective-permute-start | bytes 135176 | tf_op jit(solution)/shard_map/ppermute | solution.py:466
  5.9 6.5 %collective-permute-start.1 = (f32[88,128]{1,0:T(8,128)S(1)}, f32[88,128]{1,0:T(8,128)S(1)}, u32[]{:S(2)}, u32[]{:S(2)}) collective-permute-start(f32[88,128]{1,0:T(8,128)S(1)} %get-tuple-element.20), channel_id=1, source_target_pairs={{0,248},{8,0},{16,8},{24,16},{32,24},{40,32},{48,40},{56,48},{64,5... | collective-permute-start | bytes 135176 | tf_op jit(solution)/shard_map/ppermute | solution.py:466
  12.4 0.0 collective-permute-start.2
  12.4 5.7 %collective-permute-start.3 = (f32[88,128]{1,0:T(8,128)S(1)}, f32[88,128]{1,0:T(8,128)S(1)}, u32[]{:S(2)}, u32[]{:S(2)}) collective-permute-start(f32[88,128]{1,0:T(8,128)S(1)} %get-tuple-element.22), channel_id=1, source_target_pairs={{0,240},{8,248},{16,0},{24,8},{32,16},{40,24},{48,32},{56,40},{64,... | collective-permute-start | bytes 135176 | tf_op jit(solution)/shard_map/ppermute | solution.py:466
  18.1 0.0 collective-permute-start.4
  18.1 0.0 copy-done.8
  18.1 0.0 copy-start.6
  18.1 0.1 copy.13.cg_ref
  18.2 0.0 copy-done
  18.2 0.0 copy-done.2
  18.2 0.0 copy-done.3
  18.2 0.0 copy-done.1
  18.2 0.6 %copy-done.6 = f32[1024]{0:T(1024)S(1)} copy-done((f32[1024]{0:T(1024)S(1)}, f32[1024]{0:T(1024)}, u32[]{:S(2)}) %copy-start.6) | copy-done | bytes 4120
  18.8 0.0 copy-done.7
  18.8 0.1 copy-done.5
  18.9 0.0 copy-done.4
  18.9 4.5 %local_slots.1 = (f32[168,1024]{1,0:T(8,128)S(1)}, f32[168,1024]{1,0:T(8,128)S(1)}, f32[168,1024]{1,0:T(8,128)S(1)}, f32[168,128]{1,0:T(8,128)S(1)}, f32[2,8,1024]{2,1,0:T(8,128)S(1)}, /*index=5*/s32[8,1024]{1,0:T(8,128)S(1)}) custom-call(f32[168,1024]{1,0:T(8,128)S(1)} %get-tuple-element.24.x_ref, s32[88,1024]{1,0:T(8,128)S(1)} %get-tuple-element.25.packed, ...), custom_call_target="tpu_custom_call" | custom-call | flops 20000000 | bytes 4000000 | tf_op jit(solution)/shard_map/local_slots/pallas_call | solution.py:469
  23.4 0.0 collective-permute-done.g0
  23.4 0.0 collective-permute-done.1.g1
  23.4 0.0 collective-permute-done.2.g2
  23.4 0.0 collective-permute-done.3.g3
  23.4 0.0 collective-permute-done.4.g4
  23.4 2.3 %ghost_slots.1 = (f32[168,1024]{1,0:T(8,128)S(1)}, f32[8,16,128]{2,1,0:T(8,128)S(1)}) custom-call(f32[88,128]{1,0:T(8,128)S(1)} %collective-permute-done.g0, f32[88,128]{1,0:T(8,128)S(1)} %collective-permute-done.1.g1, f32[88,128]{1,0:T(8,128)S(1)} %collective-permute-done.2.g2, f32[88,128]{1,0:T(8,128)S(1)} %collective-permute-done.3.g3, ...), custom_call_target="tpu_custom_call" | custom-call | tf_op jit(solution)/shard_map/ghost_slots/pallas_call | solution.py:506
  25.7 10.6 %all_to_all.5.sums_ref = f32[8,16,128]{2,1,0:T(8,128)S(1)} all-to-all(f32[8,16,128]{2,1,0:T(8,128)S(1)} %get-tuple-element.31), channel_id=1, replica_groups=mesh['space'=32,'spec'=8] {'spec'}, dimensions={0} | all-to-all | bytes 131072 | tf_op jit(solution)/shard_map/all_to_all | solution.py:521
  36.3 1.5 %source.1 = (f32[162,1024]{1,0:T(8,128)}, f32[1,128]{1,0:T(1,128)}) custom-call(f32[8,16,128]{2,1,0:T(8,128)S(1)} %all_to_all.5.sums_ref, f32[168,1024]{1,0:T(8,128)S(1)} %get-tuple-element.32.adv_ref, f32[168,1024]{1,0:T(8,128)S(1)} %get-tuple-element.33.wind_ref, f32[168,128]{1,0:T(8,128)S(1)} %get-tuple-element.28.fc_ref), custom_call_target="tpu_custom_call" | custom-call | tf_op jit(solution)/shard_map/source/pallas_call | solution.py:522
  (3 shorter events, 0.0 us)
Async XLA Ops:
  1.4 16.7 %copy-start.8 = (f32[36,32]{0,1:T(8,128)S(1)}, f32[36,32]{0,1:T(8,128)}, u32[]{:S(2)}) copy-start(f32[36,32]{0,1:T(8,128)} %param.14) | copy-start | bytes 13828
  1.4 16.8 %copy-start = (f32[184,128]{1,0:T(8,128)S(1)}, f32[184,128]{1,0:T(8,128)}, u32[]{:S(2)}) copy-start(f32[184,128]{1,0:T(8,128)} %constant.4.clone.tab_ref) | copy-start | bytes 282628
  1.4 16.8 %copy-start.2 = (f32[8,1024]{1,0:T(8,128)S(1)}, f32[8,1024]{1,0:T(8,128)}, u32[]{:S(2)}) copy-start(f32[8,1024]{1,0:T(8,128)} %ew_ref.1) | copy-start | bytes 98308
  1.4 16.8 %copy-start.3 = (f32[8,1024]{1,0:T(8,128)S(1)}, f32[8,1024]{1,0:T(8,128)}, u32[]{:S(2)}) copy-start(f32[8,1024]{1,0:T(8,128)} %ea_ref.1) | copy-start | bytes 98308
  3.3 14.9 %copy-start.1 = (s32[8,1024]{1,0:T(8,128)S(1)}, s32[8,1024]{1,0:T(8,128)}, u32[]{:S(2)}) copy-start(s32[8,1024]{1,0:T(8,128)} %nb_ref.1) | copy-start | bytes 98308
  3.3 20.0 %collective-permute-start = (f32[88,128]{1,0:T(8,128)S(1)}, f32[88,128]{1,0:T(8,128)S(1)}, u32[]{:S(2)}, u32[]{:S(2)}) collective-permute-start(f32[88,128]{1,0:T(8,128)S(1)} %get-tuple-element.19), channel_id=1, source_target_pairs={{0,8},{8,16},{16,24},{24,32},{32,40},{40,48},{48,56},{56,64},{64,7... | collective-permute-start | bytes 135176 | tf_op jit(solution)/shard_map/ppermute | solution.py:466
  5.9 17.5 %collective-permute-start.1 = (f32[88,128]{1,0:T(8,128)S(1)}, f32[88,128]{1,0:T(8,128)S(1)}, u32[]{:S(2)}, u32[]{:S(2)}) collective-permute-start(f32[88,128]{1,0:T(8,128)S(1)} %get-tuple-element.20), channel_id=1, source_target_pairs={{0,248},{8,0},{16,8},{24,16},{32,24},{40,32},{48,40},{56,48},{64,5... | collective-permute-start | bytes 135176 | tf_op jit(solution)/shard_map/ppermute | solution.py:466
  12.4 11.0 %collective-permute-start.2 = (f32[88,128]{1,0:T(8,128)S(1)}, f32[88,128]{1,0:T(8,128)S(1)}, u32[]{:S(2)}, u32[]{:S(2)}) collective-permute-start(f32[88,128]{1,0:T(8,128)S(1)} %get-tuple-element.21), channel_id=1, source_target_pairs={{0,16},{8,24},{16,32},{24,40},{32,48},{40,56},{48,64},{56,72},{64,... | collective-permute-start | bytes 135176 | tf_op jit(solution)/shard_map/ppermute | solution.py:466
  12.4 11.0 %collective-permute-start.3 = (f32[88,128]{1,0:T(8,128)S(1)}, f32[88,128]{1,0:T(8,128)S(1)}, u32[]{:S(2)}, u32[]{:S(2)}) collective-permute-start(f32[88,128]{1,0:T(8,128)S(1)} %get-tuple-element.22), channel_id=1, source_target_pairs={{0,240},{8,248},{16,0},{24,8},{32,16},{40,24},{48,32},{56,40},{64,... | collective-permute-start | bytes 135176 | tf_op jit(solution)/shard_map/ppermute | solution.py:466
  18.1 5.4 %collective-permute-start.4 = (f32[88,128]{1,0:T(8,128)S(1)}, f32[88,128]{1,0:T(8,128)S(1)}, u32[]{:S(2)}, u32[]{:S(2)}) collective-permute-start(f32[88,128]{1,0:T(8,128)S(1)} %get-tuple-element.23), channel_id=1, source_target_pairs={{0,128},{8,136},{16,144},{24,152},{32,160},{40,168},{48,176},{56,1... | collective-permute-start | bytes 135176 | tf_op jit(solution)/shard_map/ppermute | solution.py:466
  18.1 0.7 %copy-start.6 = (f32[1024]{0:T(1024)S(1)}, f32[1024]{0:T(1024)}, u32[]{:S(2)}) copy-start(f32[1024]{0:T(1024)} %param.19) | copy-start | bytes 12292
  18.1 0.7 %copy-start.7 = (f32[1024]{0:T(1024)S(1)}, f32[1024]{0:T(1024)}, u32[]{:S(2)}) copy-start(f32[1024]{0:T(1024)} %param.20) | copy-start | bytes 12292
  18.2 0.7 %copy-start.5 = (s32[1024]{0:T(1024)S(1)}, s32[1024]{0:T(1024)}, u32[]{:S(2)}) copy-start(s32[1024]{0:T(1024)} %param.13) | copy-start | bytes 12292
  18.2 0.7 %copy-start.4 = (s32[1024]{0:T(1024)S(1)}, s32[1024]{0:T(1024)}, u32[]{:S(2)}) copy-start(s32[1024]{0:T(1024)} %param.12) | copy-start | bytes 12292
